TPU v7x, 256 devices: a whole 4x4x8 slice. The times are simulated.
256 devices in a mesh: seed: 2 (over core), px: 16 (over y_lo, z), py: 8 (over x, y_hi).
Axes of the slice: x: 4, y: 4 (y_hi: 2, y_lo: 2; y = y_hi * 2 + y_lo), z: 8, core: 2. Of those that a mesh axis runs over, the one named last changes fastest.
Arguments:
- input_field: float32 [1, 3, 128, 128, 128], P(None, None, 'px', 'py'), may hold values from -6 to 6
- target_field: float32 [1, 3, 128, 128, 128], P(None, None, 'px', 'py'), may hold values from -6 to 6
- row_mask: int32 [256, 128], P(('seed', 'px'), 'py'), parts along dimension 0, may hold values from 0 to 2
- modes: int32 [6, 32], P('seed'), parts along dimension 0, may hold values from 0 to 127, as said below
- lift_weight: float32 [64, 3], P('seed'), parts along dimension 0, may hold values from -3.5 to 3.5
- mix_weight: float32 [64, 32], P('seed'), parts along dimension 0, may hold values from -1 to 1
- spectral_weight: float32 [4, 32, 32, 32, 1024], P('seed', 'py', None, 'px'), parts along dimension 0, may hold values from -8 to 8
- proj_weight: float32 [6, 32], P('seed'), parts along dimension 0, may hold values from -1 to 1
Outputs:
- lift_grad: float32 [64, 3], P('seed'), parts along dimension 0
- mix_grad: float32 [64, 32], P('seed'), parts along dimension 0
- proj_grad: float32 [6, 32], P('seed'), parts along dimension 0
- spectral_grad: float32 [4, 32, 32, 32, 1024], P('seed', 'py', None, 'px'), parts along dimension 0
There are 2 independent parts, one for each index of `seed`. A program takes and returns all parts, laid end to end along the dimension named above; an argument that names none is the same for every part. Nothing has to cross between parts.
Inputs may be any that keep to these rules, and one draw needn't show every extreme that they name: `modes`: each row holds the usual Fourier neural operator truncation of one grid dimension: the frequencies 0 .. 15 and 112 .. 127, each once, in an order drawn from the seed.
All inputs are finite; a program needn't handle non-finite values.
Results may differ from a plain program's by a relative error of at most 0.00021.
Values sent between devices are 32-bit elements; how exact they have to be, the bound alone decides.
No kernel may reach another device: no remote copies, remote signals or barrier semaphores. Data moves between devices by JAX's collectives and lax.ppermute only.
A program may use at most 128 MiB of HBM per device.

v0:
```python
import math

import jax
import jax.numpy as jnp
from jax import lax
from jax.sharding import PartitionSpec as P

C = 32
N = 128
M = 32


HIGHEST = lax.Precision.HIGHEST


def contract(pattern, left, right):
    return jnp.einsum(pattern, left, right, precision=HIGHEST)


def tables(frequency, length):
    places = jnp.arange(length, dtype=jnp.int32)
    turn_count = places[:, None] * frequency[None, :] % length
    angles = turn_count.astype(jnp.float32) * jnp.float32(2.0 * math.pi / length)
    return (jnp.cos(angles), jnp.sin(angles))


def forward(fields, waves):
    x_cos, x_sin, y_cos, y_sin, z_cos, z_sin = waves
    count, depth, x_local, y_local, length = fields.shape
    real_z = contract("bkxyn,nr->rbxyk", fields, z_cos)
    imag_z = -contract("bkxyn,nr->rbxyk", fields, z_sin)
    along_z = jnp.stack([real_z, imag_z], axis=2).reshape((M, count, 2, x_local, y_local * depth))

    def along_y(pieces):
        shape_now = pieces.shape
        split = pieces.reshape(shape_now[:4] + (N, depth))
        real_part = split[:, :, 0]
        imag_part = split[:, :, 1]
        new_real = contract("rbpyk,yq->rbpqk", real_part, y_cos) + contract(
            "rbpyk,yq->rbpqk", imag_part, y_sin
        )
        new_imag = contract("rbpyk,yq->rbpqk", imag_part, y_cos) - contract(
            "rbpyk,yq->rbpqk", real_part, y_sin
        )
        return jnp.stack([new_real, new_imag], axis=2)

    pieces = lax.all_to_all(along_z, "px", split_axis=0, concat_axis=3, tiled=True)
    real_part = pieces[:, :, 0]
    imag_part = pieces[:, :, 1]
    new_real = contract("rbxK,xp->rbpK", real_part, x_cos) + contract(
        "rbxK,xp->rbpK", imag_part, x_sin
    )
    new_imag = contract("rbxK,xp->rbpK", imag_part, x_cos) - contract(
        "rbxK,xp->rbpK", real_part, x_sin
    )
    first_pass = jnp.stack([new_real, new_imag], axis=2)
    return along_y(lax.all_to_all(first_pass, "py", split_axis=3, concat_axis=4, tiled=True))


def inverse(spectrum, waves, scaling, y_local):
    x_cos, x_sin, y_cos, y_sin, z_cos, z_sin = waves
    r_local, count, two, p_local, q_count, depth = spectrum.shape
    real_part = spectrum[:, :, 0]
    imag_part = spectrum[:, :, 1]
    real_y = contract("rbpqk,yq->rbpyk", real_part, y_cos) - contract(
        "rbpqk,yq->rbpyk", imag_part, y_sin
    )
    imag_y = contract("rbpqk,yq->rbpyk", imag_part, y_cos) + contract(
        "rbpqk,yq->rbpyk", real_part, y_sin
    )
    along_y = jnp.stack([real_y, imag_y], axis=2).reshape((r_local, count, 2, p_local, N * depth))
    pieces = lax.all_to_all(along_y, "py", split_axis=4, concat_axis=3, tiled=True)
    real_in = pieces[:, :, 0]
    imag_in = pieces[:, :, 1]
    new_real = contract("rbpK,xp->rbxK", real_in, x_cos) - contract("rbpK,xp->rbxK", imag_in, x_sin)
    new_imag = contract("rbpK,xp->rbxK", imag_in, x_cos) + contract("rbpK,xp->rbxK", real_in, x_sin)
    second_pass = jnp.stack([new_real, new_imag], axis=2)
    pieces = lax.all_to_all(second_pass, "px", split_axis=3, concat_axis=0, tiled=True)
    shape_now = pieces.shape
    split = pieces.reshape(shape_now[:4] + (y_local, depth))
    return scaling * (
        contract("rbxyk,nr->bkxyn", split[:, :, 0], z_cos)
        - contract("rbxyk,nr->bkxyn", split[:, :, 1], z_sin)
    )


def unfold(flat_weights):
    return flat_weights.reshape(flat_weights.shape[:4] + (C, C))


def mix_modes(weights, spectrum):
    first = spectrum[:, :, 0]
    second = spectrum[:, :, 1]
    real_part = contract("rbpqi,pqrio->rbpqo", first, weights[0]) - contract(
        "rbpqi,pqrio->rbpqo", second, weights[1]
    )
    imag_part = contract("rbpqi,pqrio->rbpqo", second, weights[0]) + contract(
        "rbpqi,pqrio->rbpqo", first, weights[1]
    )
    return jnp.stack([real_part, imag_part], axis=2)


def mix_back(weights, spectrum, incoming):
    first = spectrum[:, :, 0]
    second = spectrum[:, :, 1]
    grad_real = incoming[:, :, 0]
    grad_imag = incoming[:, :, 1]
    weight_real = contract("rbpqi,rbpqo->pqrio", first, grad_real) + contract(
        "rbpqi,rbpqo->pqrio", second, grad_imag
    )
    weight_imag = contract("rbpqi,rbpqo->pqrio", first, grad_imag) - contract(
        "rbpqi,rbpqo->pqrio", second, grad_real
    )
    modes_real = contract("rbpqo,pqrio->rbpqi", grad_real, weights[0]) + contract(
        "rbpqo,pqrio->rbpqi", grad_imag, weights[1]
    )
    modes_imag = contract("rbpqo,pqrio->rbpqi", grad_imag, weights[0]) - contract(
        "rbpqo,pqrio->rbpqi", grad_real, weights[1]
    )
    return (jnp.stack([weight_real, weight_imag]), jnp.stack([modes_real, modes_imag], axis=2))


def body(
    input_field,
    target_field,
    row_mask,
    modes,
    lift_weight,
    mix_weight,
    spectral_weight,
    proj_weight,
):
    waves = tables(modes[0], N) + tables(modes[1], N) + tables(modes[2], N)
    cells = float(N**3)
    y_local = input_field.shape[3]
    square_weights = unfold(spectral_weight)
    lifted = contract("cj,bjxyn->bcxyn", lift_weight, input_field)
    lifted_modes = forward(lifted, waves)
    spectral = inverse(mix_modes(square_weights, lifted_modes), waves, 1.0 / cells, y_local)
    preact = contract("cd,bdxyn->bcxyn", mix_weight, lifted) + spectral
    active, gelu_back = jax.vjp(jax.nn.gelu, preact)
    output_field = contract("jc,bcxyn->bjxyn", proj_weight, active)
    weights_mask = row_mask.astype(jnp.float32)[None, None, :, :, None]
    out_grad = 2.0 * weights_mask * (output_field - target_field)
    proj_grad = contract("bjxyn,bcxyn->jc", out_grad, active)
    preact_grad = gelu_back(contract("jc,bjxyn->bcxyn", proj_weight, out_grad))[0]
    mix_grad = contract("bcxyn,bdxyn->cd", preact_grad, lifted)
    mixed_grad = forward(preact_grad, waves) / cells
    square_grad, modes_grad = mix_back(square_weights, lifted_modes, mixed_grad)
    spectral_grad = square_grad.reshape(spectral_weight.shape)
    lifted_grad = contract("dc,bdxyn->bcxyn", mix_weight, preact_grad)
    lifted_grad = lifted_grad + inverse(modes_grad, waves, 1.0, y_local)
    lift_grad = contract("bcxyn,bjxyn->cj", lifted_grad, input_field)
    lift_total, mix_total, proj_total = lax.psum((lift_grad, mix_grad, proj_grad), ("px", "py"))
    return (lift_total / cells, mix_total / cells, proj_total / cells, spectral_grad)


def solution(mesh):
    in_specs = (
        P(None, None, "px", "py", None),
        P(None, None, "px", "py", None),
        P(("seed", "px"), "py"),
        P("seed", None),
        P("seed", None),
        P("seed", None),
        P("seed", "py", None, "px", None),
        P("seed", None),
    )
    out_specs = (
        P("seed", None),
        P("seed", None),
        P("seed", None),
        P("seed", "py", None, "px", None),
    )
    return jax.shard_map(body, mesh=mesh, in_specs=in_specs, out_specs=out_specs, check_vma=False)
```

profile of v0, /device:TPU:128, one launch (start us, length us, event | category | flops | bytes accessed | tf_op | source)
XLA Modules:
  0.0 1176.8 jit_solution(8642196237942819875)
XLA Ops:
  4.2 9.7 fusion.45
  13.9 11.3 negate_bitcast_fusion.1
  30.0 4.2 copy.60
  36.7 31.5 %all_to_all.132 = f32[32,1,2,8,512]{4,3,2,1,0:T(8,128)S(1)} all-to-all(f32[32,1,2,8,512]{4,3,2,1,0:T(8,128)S(1)} %copy.61), channel_id=1, replica_groups=mesh['seed'=2,'px'=16,'py'=8] {'px'}, dimensions={0} | all-to-all | bytes 2097152 | tf_op jit(solution)/shard_map/all_to_all | solution.py:47
  71.3 6.6 all-to-all-start.1
  77.9 3.4 fusion.384
  81.3 4.2 squeeze.4
  92.9 5.5 fusion.12
  98.4 3.4 fusion.14
  101.9 3.4 fusion.4
  105.3 3.4 fusion.6
  112.2 8.3 copy.69
  120.5 14.3 %reshape.407 = f32[8,1,8192]{2,1,0:T(1,128)S(1)} reshape(f32[4096,1,2,2,4]{4,3,2,1,0:T(2,128)} %bitcast.565) | data formatting | bytes 524288
  134.8 15.4 %all_to_all.133 = f32[8,1,8192]{2,1,0:T(1,128)S(1)} all-to-all(f32[8,1,8192]{2,1,0:T(1,128)S(1)} %reshape.407), channel_id=1, replica_groups=mesh['seed'=2,'px'=16,'py'=8] {'py'}, dimensions={0} | all-to-all | bytes 524288 | tf_op jit(solution)/shard_map/all_to_all | solution.py:72
  152.0 16.0 %reshape.408 = f32[4096,1,2,2,4]{4,3,2,1,0:T(2,128)} reshape(f32[8,8192]{1,0:T(8,128)S(1)} %reduce) | data formatting | bytes 524288
  168.0 6.8 copy.125
  180.1 7.9 all-to-all-start.3
  188.1 20.5 %all-to-all-done.3 = f32[2,1,2,128,512]{4,0,2,1,3:T(2,128)S(1)} async-done(((f32[2,1,2,128,512]{4,0,2,1,3:T(2,128)}), f32[2,1,2,128,512]{4,0,2,1,3:T(2,128)S(1)}, u32[]{:S(2)}, u32[]{:S(2)}) %all-to-all-start.3) | async-done | bytes 1048608 | tf_op jit(solution)/shard_map/all_to_all | solution.py:78
  213.8 4.8 fusion.383
  218.5 3.2 copy.131
  221.8 4.9 fusion.208
  226.6 3.2 copy.130
  229.9 3.7 fusion.202
  240.8 10.0 negate_bitcast_fusion
  250.8 11.0 convolution_bitcast_fusion
  266.7 4.1 copy.78
  273.3 29.4 %all_to_all.134 = f32[32,1,2,8,512]{4,3,2,1,0:T(8,128)S(1)} all-to-all(f32[32,1,2,8,512]{4,3,2,1,0:T(8,128)S(1)} %copy.80), channel_id=1, replica_groups=mesh['seed'=2,'px'=16,'py'=8] {'px'}, dimensions={0} | all-to-all | bytes 2097152 | tf_op jit(solution)/shard_map/all_to_all | solution.py:47
  305.1 12.3 %all_to_all.135 = f32[2,1,2,32,512]{4,0,2,1,3:T(2,128)S(1)} all-to-all(f32[2,1,2,32,512]{4,0,2,1,3:T(2,128)S(1)} %copy.82), channel_id=1, replica_groups=mesh['seed'=2,'px'=16,'py'=8] {'py'}, dimensions={3} | all-to-all | bytes 524288 | tf_op jit(solution)/shard_map/all_to_all | solution.py:57
  322.3 6.6 fusion.10
  328.9 7.0 fusion
  335.9 6.6 fusion.8
  342.5 6.6 fusion.2
  352.4 8.4 copy.88
  360.8 14.3 %reshape.409 = f32[8,1,8192]{2,1,0:T(1,128)S(1)} reshape(f32[4096,1,2,2,4]{4,3,2,1,0:T(2,128)} %bitcast.567) | data formatting | bytes 524288
  375.1 11.3 all_to_all.136
  387.6 16.0 %reshape.410 = f32[4096,1,2,2,4]{4,3,2,1,0:T(2,128)} reshape(f32[8,8192]{1,0:T(8,128)S(1)} %reduce.1) | data formatting | bytes 524288
  403.7 6.8 copy.127
  415.8 7.6 all-to-all-start.7
  423.7 4.2 fusion.76
  430.6 3.3 fusion.113
  434.1 4.7 multiply_add_fusion
  438.8 4.0 stack.117
  442.8 4.0 stack.118
  452.4 4.8 fusion.382
  459.4 3.3 fusion.206
  462.8 3.4 copy.134
  466.1 3.7 fusion.200
  471.9 702.7 %all-reduce = (f32[32,3]{0,1:T(4,128)S(1)}, f32[32,32]{1,0:T(8,128)S(1)}, f32[3,32]{1,0:T(4,128)S(1)}) all-reduce(f32[32,3]{0,1:T(4,128)S(1)} %fusion.82, f32[32,32]{1,0:T(8,128)S(1)} %copy-done.20, f32[3,32]{1,0:T(4,128)S(1)} %copy-done.24), channel_id=1, replica_groups=mesh['seed'=2,'px'=16,'py'=8] {'px','py'}, use_global_device_ids=true, to_apply=%region_0.1 | all-reduce | flops 1216 | bytes 9728 | tf_op jit(solution)/shard_map/psum | solution.py:154
  (165 shorter events, 82.6 us)
Async XLA Ops:
  0.6 233.0 %copy-start = (f32[32,32]{1,0:T(8,128)S(1)}, f32[32,32]{1,0:T(8,128)}, u32[]{:S(2)}) copy-start(f32[32,32]{1,0:T(8,128)} %param.13) | copy-start | bytes 12292
  1.4 249.4 %copy-start.21 = (s32[32]{0:T(128)}, s32[32]{0:T(128)S(1)}, u32[]{:S(2)}) copy-start(s32[32]{0:T(128)S(1)} %get-tuple-element.20) | copy-start | bytes 388
  1.4 302.9 %copy-start.18 = (s32[32]{0:T(128)}, s32[32]{0:T(128)S(1)}, u32[]{:S(2)}) copy-start(s32[32]{0:T(128)S(1)} %get-tuple-element.21) | copy-start | bytes 388
  1.4 319.6 %copy-start.16 = (s32[32]{0:T(128)}, s32[32]{0:T(128)S(1)}, u32[]{:S(2)}) copy-start(s32[32]{0:T(128)S(1)} %get-tuple-element.19) | copy-start | bytes 388
  71.3 17.4 %all-to-all-start.1 = ((f32[2,1,2,32,512]{4,0,2,1,3:T(2,128)}), f32[2,1,2,32,512]{4,0,2,1,3:T(2,128)S(1)}, u32[]{:S(2)}, u32[]{:S(2)}) async-start(f32[2,1,2,32,512]{4,0,2,1,3:T(2,128)} %copy.63), calls=%async_computation.1 | async-start | bytes 524288 | tf_op jit(solution)/shard_map/all_to_all | solution.py:57
  88.7 0.7 copy-start.14
  92.8 5.5 copy-start.1
  98.4 3.5 copy-start.3
  178.4 9.7 copy-start.23
  180.1 28.5 %all-to-all-start.3 = ((f32[2,1,2,128,512]{4,0,2,1,3:T(2,128)}), f32[2,1,2,128,512]{4,0,2,1,3:T(2,128)S(1)}, u32[]{:S(2)}, u32[]{:S(2)}) async-start(f32[2,1,2,128,512]{4,0,2,1,3:T(2,128)} %copy.72), calls=%async_computation.3 | async-start | bytes 2097152 | tf_op jit(solution)/shard_map/all_to_all | solution.py:78
  208.6 1.0 copy-start.10
  229.8 3.7 copy-start.9
  233.6 2.2 copy-start.25
  233.6 2.2 copy-start.26
  235.8 1.8 copy-start.11
  237.7 3.1 copy-start.27
  240.8 10.1 copy-start.5
  319.4 2.8 copy-start.2
  322.3 6.6 copy-start.4
  342.5 7.1 copy-start.17
  403.7 7.1 copy-start.19
  415.8 33.4 %all-to-all-start.7 = ((f32[2,1,2,128,512]{4,0,2,1,3:T(2,128)}), f32[2,1,2,128,512]{4,0,2,1,3:T(2,128)S(1)}, u32[]{:S(2)}, u32[]{:S(2)}) async-start(f32[2,1,2,128,512]{4,0,2,1,3:T(2,128)} %copy.91), calls=%async_computation.7 | async-start | bytes 2097152 | tf_op jit(solution)/shard_map/all_to_all | solution.py:78
  423.7 4.2 copy-start.12
  423.7 4.2 copy-start.28
  427.9 2.7 copy-start.6
  430.6 3.3 copy-start.15
  457.2 2.3 copy-start.22
  462.8 7.1 copy-start.13
  466.1 3.8 copy-start.7
  466.1 3.8 copy-start.8
  469.9 2.0 copy-start.20
  469.9 1.9 copy-start.24
where the time goes:
time: 1190 us; the launch traced here: 1180 us
  blocking collectives  803 us (67%)
  local copies, waits for them, and re-layouts  178 us (15%)
  matrix products  140 us (12%)
  starting transfers between devices  22.2 us (2%)
  waiting for transfers between devices  20.5 us (2%)
  other arithmetic  11.9 us (1%)
    psum x1, blocking collectives, body(): lax.psum((lift_grad, mix_grad, proj_grad), ('px', 'py'))  703 us
    dot_general x52, matrix products, contract(): return jnp.einsum(pattern, left, right, precision=HIGHEST)  124 us
    unnamed x66, local copies, waits for them, and re-layouts  74.5 us
    all_to_all x2, blocking collectives, forward(): lax.all_to_all(along_z, 'px', split_axis=0, concat_axis=3, tiled=True)  60.9 us
    all_to_all x2, blocking collectives, inverse(): lax.all_to_all(along_y, 'py', split_axis=4, concat_axis=3, tiled=True)  26.8 us
  transfers between devices with their start and end apart: 3, of which 1 were waited for; matrix products, arithmetic and copies ran while one was open for 3% of the time, Pallas kernels for 0%

commit v1 on v0

v1 whole, which is shorter than its diff:
```python
import math

import jax
import jax.numpy as jnp
from jax import lax
from jax.experimental import pallas as pl
from jax.experimental.pallas import tpu as pltpu
from jax.sharding import PartitionSpec as P

C = 32
N = 128
M = 32
F32 = jnp.float32
BF16 = jnp.bfloat16
SCALE = 1.0 / float(N**3)
GELU_A = math.sqrt(2.0 / math.pi)
GELU_B = 0.044715

NN = (((1,), (0,)), ((), ()))
NT = (((1,), (1,)), ((), ()))


def split(value):
    high = value.astype(BF16)
    return high, (value - high.astype(F32)).astype(BF16)


def mul(left, right, dims):
    return lax.dot_general(left, right, dims, preferred_element_type=F32)


def dot3(left, right, dims=NN):
    left_high, left_low = left if isinstance(left, tuple) else split(left)
    right_high, right_low = right if isinstance(right, tuple) else split(right)
    return (
        mul(left_low, right_high, dims)
        + mul(left_high, right_low, dims)
        + mul(left_high, right_high, dims)
    )


def iota(shape, axis):
    return lax.broadcasted_iota(jnp.int32, shape, axis)


def wave(turns):
    place = jnp.abs((turns & (N - 1)) - N // 2).astype(F32)
    angle = (place - N / 4) * (2.0 * math.pi / N)
    square = angle * angle
    series = 1.0 / 39916800.0
    for term in (362880.0, 5040.0, 120.0, 6.0, 1.0):
        series = 1.0 / term - square * series
    return angle * series


def regroup(pieces):
    group = iota(pieces[0].shape, 1) // 16
    out = []
    for target in range(8):
        total = pieces[target]
        for source in range(8):
            if source != target:
                moved = pltpu.roll(pieces[source], (16 * (source - target)) % 128, 1)
                total = jnp.where(group == source, moved, total)
        out.append(total)
    return out


def depth_waves(freq_ref):
    shape = (N, 128)
    lane = iota(shape, 1)
    return wave(iota(shape, 0) * freq_ref[2:3, :] + 32 * (lane & 1))


def input_depth(freq_ref, field_ref, out_ref):
    table = split(depth_waves(freq_ref).T[:64])
    lane = iota((32, 128), 1)
    blank = jnp.zeros((16, N), F32)
    for x in range(8):
        rows = [field_ref[channel, x] for channel in range(3)] + [blank]
        both = jnp.concatenate(rows + rows, axis=0)
        result = dot3(table, both, NT)
        out_ref[pl.ds(x, 32, stride=8), :] = jnp.where(lane < 64, result[:32], result[32:])


def rows_waves(freq_row, phase):
    shape = (256, 128)
    row = iota(shape, 0)
    place = (row // 16) * 8 + row % 8
    return place * freq_row + phase(row // 8 % 2)


def input_rows(freq_ref, pieces_ref, out_ref):
    lane = iota((256, 128), 1)
    table = wave(rows_waves(freq_ref[4:5, :], lambda part: 32 * ((lane // 4) % 2 - part)))
    out_ref[...] = dot3(table.T[:64], pieces_ref[...])


def mix_kernel(freq_ref, pieces_ref, lift_ref, weight_ref, modes_ref, out_ref, held_ref):
    pieces = [pieces_ref[8 * source : 8 * source + 8, :] for source in range(8)]
    group = iota((8, 128), 1) // 16
    rows = jnp.concatenate(regroup(pieces), axis=0)
    shape = (N, 128)
    lane = iota(shape, 1)
    turns = iota(shape, 0) * freq_ref[1:2, :]
    left = wave(turns + 32 * (lane // 64))
    right = wave(turns + 32 * (lane // 64) - 32)
    rows = split(rows)
    held_ref[:, :128] = dot3(rows, left)
    held_ref[:, 128:] = dot3(rows, right)
    even = iota((4, 128), 1) % 2 == 0
    modes_ref[...] = jnp.zeros((32, 128), F32)
    for channel in range(3):
        both = []
        for parity in range(2):
            base = 8 * (4 * parity + channel)
            both.append(held_ref[base : base + 4, :128] + held_ref[base + 4 : base + 8, 128:])
        modes_ref[pl.ds(channel, 4, stride=8), :] = jnp.where(even, both[0], both[1])
    lift = split(lift_ref[...])
    fold = jnp.where(iota((32, 1024), 0) == iota((32, 1024), 1) % 32, SCALE, 0.0).astype(BF16)
    for p in range(4):
        spread = dot3(modes_ref[8 * p : 8 * p + 8, :].T, lift)
        real, imag = spread[:64], spread[64:]
        first, second = weight_ref[0, p], weight_ref[1, p]
        product = jnp.concatenate([first * real - second * imag, second * real + first * imag], axis=0)
        high, low = split(product)
        mixed = mul(fold, low, NT) + mul(fold, high, NT)
        for target in range(8):
            start = 8 * (target // 2)
            out_ref[target, p] = mixed[start : start + 8]


def expand(freq_ref, pieces_ref, out_ref, held_ref):
    shape = (256, 128)
    row, lane = iota(shape, 0), iota(shape, 1)
    table = wave((row % 128) * freq_ref[1:2, :] + 32 * (lane // 64 - row // 128))
    table = jnp.where(freq_ref[3:4, :] == 1, table, 0.0)
    result = dot3(pieces_ref[...], table, NT)
    held_ref[:256, :] = result[:, :128]
    held_ref[256:, :] = result[:, 128:]
    parts = []
    for part in range(2):
        pieces = [held_ref[pl.ds(256 * part + o, 32, stride=8), :] for o in range(8)]
        parts.append(regroup(pieces))
    table = split(wave(rows_waves(freq_ref[0:1, :], lambda part: 32 * (lane // 32 - part)))[:, :64])
    for pair in range(4):
        wide = jnp.concatenate(
            [
                jnp.concatenate([parts[part][2 * pair + k] for part in range(2)], axis=0)
                for k in range(2)
            ],
            axis=1,
        )
        result = dot3(table, wide)
        for k in range(2):
            start = 256 * (2 * pair + k)
            out_ref[start : start + 256, :] = result[:, 128 * k : 128 * k + 128]


def grid_kernel(
    freq_ref, pieces_ref, field_ref, target_ref, mask_ref, point_ref, proj_ref, out_ref, small_ref,
    point_grad, proj_grad,
):
    waves = depth_waves(freq_ref).T[:64]
    point = point_ref[...]
    proj = split(proj_ref[...])
    blank = jnp.zeros((16, N), F32)
    empty = jnp.zeros((64, N), F32)
    point_grad[...] = jnp.zeros_like(point_grad)
    proj_grad[...] = jnp.zeros_like(proj_grad)

    def plane(x, carry):
        rows = [field_ref[channel, x] for channel in range(3)] + [blank]
        stack = jnp.concatenate([waves] + rows, axis=0)
        aims = [target_ref[channel, x] for channel in range(3)] + [blank, empty]
        aim = jnp.concatenate(aims, axis=0).T
        coefs = [pieces_ref[pl.ds(512 * o + x, 64, stride=8), :] for o in range(4)]
        coefs = jnp.concatenate([jnp.concatenate(coefs, axis=1), point], axis=0)
        preact = dot3(stack.T, coefs)
        cube = preact * preact
        bend = jnp.tanh(GELU_A * preact * (1.0 + GELU_B * cube))
        half = 0.5 * (1.0 + bend)
        active = preact * half
        slope = half + 0.5 * preact * (1.0 - bend * bend) * (
            GELU_A + (3.0 * GELU_A * GELU_B) * cube
        )
        active = split(active)
        error = mask_ref[pl.ds(x, 1), :] * (dot3(active, proj, NT) - aim)
        rate = dot3(error, proj) * slope
        both = dot3(stack, rate)
        for o in range(4):
            out_ref[pl.ds(512 * o + x, 64, stride=8), :] = both[:64, 128 * o : 128 * o + 128]
        point_grad[...] += both[64:]
        proj_grad[...] += dot3(error.T[:64], active)
        return carry

    lax.fori_loop(0, 8, plane, 0)
    same = iota((64, 512), 0) % 16 == iota((64, 512), 1) % 16
    pick = jnp.where(iota((8, 64), 0) == iota((8, 64), 1) // 16, 1.0, 0.0)
    total = jnp.zeros((8, 128), F32)
    for offset, ref in ((0, point_grad), (32, proj_grad)):
        kept = dot3(pick, jnp.where(same, ref[...], 0.0))
        place = jnp.where(iota((512, 128), 0) // 16 + offset == iota((512, 128), 1), 1.0, 0.0)
        total = total + dot3(kept, place)
    small_ref[...] = total


def reduce_kernel(freq_ref, pieces_ref, out_ref, held_ref):
    lane = iota((256, 128), 1)
    table = wave(rows_waves(freq_ref[0:1, :], lambda part: 32 * ((lane // 32) % 2 - part)))
    table = split(table.T[:64])
    results = [dot3(table, pieces_ref[256 * j : 256 * j + 256, :]) for j in range(8)]
    for part in range(2):
        pieces = regroup([result[32 * part : 32 * part + 32] for result in results])
        for o in range(8):
            held_ref[pl.ds(256 * part + o, 32, stride=8), :] = pieces[o]
    row = iota((256, 128), 0)
    table = wave((row % 128) * freq_ref[1:2, :] + 32 * (lane // 64 - row // 128))
    table = jnp.where(freq_ref[3:4, :] == 1, table, 0.0)
    table = split(table)
    out_ref[...] = dot3(
        jnp.concatenate([held_ref[:256, :], held_ref[256:, :]], axis=1), table
    )


def back_kernel(pieces_ref, modes_ref, lift_ref, weight_ref, small_ref, grad_ref, sum_ref):
    lift = split(lift_ref[...])
    tile = jnp.where(iota((32, 1024), 0) == iota((32, 1024), 1) % 32, SCALE, 0.0).astype(BF16)
    total = jnp.zeros((8, 1024), F32)
    for p in range(4):
        modes = modes_ref[8 * p : 8 * p + 8, :]
        spread = dot3(modes.T, lift)
        grads = jnp.concatenate(
            [pieces_ref[2 * o, p] + pieces_ref[2 * o + 1, p] for o in range(4)], axis=0
        )
        high, low = split(grads.T)
        outer = mul(low, tile, NN) + mul(high, tile, NN)
        real, imag = spread[:64], spread[64:]
        grad_real, grad_imag = outer[:64], outer[64:]
        grad_ref[0, p] = real * grad_real + imag * grad_imag
        grad_ref[1, p] = real * grad_imag - imag * grad_real
        first, second = weight_ref[0, p], weight_ref[1, p]
        back = jnp.concatenate(
            [first * grad_real + second * grad_imag, first * grad_imag - second * grad_real], axis=0
        )
        total = total + dot3(modes, back)
    place = jnp.where(iota((1024, 128), 0) // 32 + 64 == iota((1024, 128), 1), 1.0, 0.0)
    sum_ref[...] = small_ref[...] + dot3(total, place)


def call(kernel, shapes, scratch=(), name=None):
    return pl.pallas_call(
        kernel,
        out_shape=shapes,
        scratch_shapes=list(scratch),
        name=name,
        compiler_params=pltpu.CompilerParams(vmem_limit_bytes=48 * 1024 * 1024),
    )


def array(*shape):
    return jax.ShapeDtypeStruct(shape, F32)


def exchange(value, axes):
    return lax.all_to_all(value, axes, split_axis=0, concat_axis=0, tiled=True)


def spread_rows(matrix):
    padded = jnp.pad(matrix.T, ((0, 1), (0, 0)))
    eye = jnp.eye(16, dtype=F32)
    return (padded[:, None, :, None] * eye[None, :, None, :]).reshape(64, 512)


def body(
    input_field,
    target_field,
    row_mask,
    modes,
    lift_weight,
    mix_weight,
    spectral_weight,
    proj_weight,
):
    parity = lax.axis_index("py") % 2
    first, second, third = modes[0], modes[1], modes[2]
    lanes = jnp.arange(128, dtype=jnp.int32)
    depth = jnp.repeat(third.reshape(16, 2).T.reshape(32), 2)
    outer = jnp.broadcast_to(first.reshape(8, 1, 4), (8, 2, 4)).reshape(64)
    freq = jnp.stack(
        [
            jnp.tile(first, 4),
            jnp.tile(jnp.repeat(second, 2), 2),
            jnp.tile(depth, 2),
            (lanes % 2 == parity).astype(jnp.int32),
            jnp.tile(outer, 2),
            lanes,
            lanes,
            lanes,
        ]
    )
    field = input_field[0]
    target = target_field[0]
    weight = spectral_weight.reshape(2, 4, 64, 1024)
    mask = jnp.tile(2.0 * row_mask.astype(F32), (1, 8))
    lift_rows = jnp.pad(jnp.repeat(lift_weight.T, 32, axis=1), ((0, 5), (0, 0)))
    pointwise = jnp.einsum("cd,dj->cj", mix_weight, lift_weight, precision=lax.Precision.HIGHEST)
    point = spread_rows(pointwise)
    proj = jnp.pad(spread_rows(proj_weight.T), ((0, 64), (0, 0)))

    pieces = call(input_depth, array(256, 128), name="input_depth")(freq, field)
    pieces = exchange(pieces.reshape(16, 16, 128), "px").reshape(256, 128)
    pieces = call(input_rows, array(64, 128), name="input_rows")(freq, pieces)
    pieces = exchange(pieces.reshape(8, 8, 128), "py").reshape(64, 128)
    input_modes, pieces = call(
        mix_kernel,
        (array(32, 128), array(8, 4, 8, 128)),
        [pltpu.VMEM((64, 256), F32)],
        name="mix",
    )(freq, pieces, lift_rows, weight)
    pieces = exchange(pieces, "py").reshape(256, 128)
    pieces = call(expand, array(2048, 128), [pltpu.VMEM((512, 128), F32)], name="expand")(
        freq, pieces
    )
    pieces = exchange(pieces.reshape(128, 16, 128), ("py", "px")).reshape(2048, 128)
    pieces, small = call(
        grid_kernel,
        (array(2048, 128), array(8, 128)),
        [pltpu.VMEM((64, 512), F32), pltpu.VMEM((64, 512), F32)],
        name="grid",
    )(freq, pieces, field, target, mask, point, proj)
    pieces = exchange(pieces.reshape(128, 16, 128), ("py", "px")).reshape(2048, 128)
    pieces = call(reduce_kernel, array(256, 128), [pltpu.VMEM((512, 128), F32)], name="reduce")(
        freq, pieces
    )
    pieces = exchange(pieces.reshape(8, 4, 8, 128), "py")
    grad, sums = call(back_kernel, (array(2, 4, 64, 1024), array(8, 128)), name="back")(
        pieces, input_modes, lift_rows, weight, small
    )
    sums = exchange(jnp.broadcast_to(sums[None, :3], (128, 3, 128)), ("px", "py"))
    sums = jnp.sum(sums, axis=0)
    cross, proj_total, lift_part = sums[:, :32], sums[:, 32:64], sums[:, 64:96]
    high = lax.Precision.HIGHEST
    lift_total = jnp.einsum("dc,jd->cj", mix_weight, cross, precision=high) + lift_part.T
    mix_total = jnp.einsum("jc,dj->cd", cross, lift_weight, precision=high)
    return (
        lift_total * SCALE,
        mix_total * SCALE,
        proj_total * SCALE,
        grad.reshape(spectral_weight.shape),
    )


def solution(mesh):
    in_specs = (
        P(None, None, "px", "py", None),
        P(None, None, "px", "py", None),
        P(("seed", "px"), "py"),
        P("seed", None),
        P("seed", None),
        P("seed", None),
        P("seed", "py", None, "px", None),
        P("seed", None),
    )
    out_specs = (
        P("seed", None),
        P("seed", None),
        P("seed", None),
        P("seed", "py", None, "px", None),
    )
    return jax.shard_map(body, mesh=mesh, in_specs=in_specs, out_specs=out_specs, check_vma=False)
```

time: 1190 us -> 174 us (0.15)
  the two profiles are of different devices: /device:TPU:128 before, /device:TPU:8 now
where the time goes in v1:
time: 174 us; the launch traced here: 173 us
  blocking collectives  73.4 us (42%)
  waiting for transfers between devices  33.3 us (19%)
  local copies, waits for them, and re-layouts  20.6 us (12%)
  starting transfers between devices  20.4 us (12%)
  Pallas kernels  20.2 us (12%)
  other arithmetic  2.45 us (1%)
    all_to_all x4, blocking collectives, exchange(): return lax.all_to_all(value, axes, split_axis=0, concat_axis=0, tiled=True)  73.4 us
    all_to_all x3, waiting for transfers between devices, exchange(): return lax.all_to_all(value, axes, split_axis=0, concat_axis=0, tiled=True)  33.3 us
    all_to_all x3, starting transfers between devices, exchange(): return lax.all_to_all(value, axes, split_axis=0, concat_axis=0, tiled=True)  20.4 us
    pallas_call x1, Pallas kernels, body(): call(grid_kernel, (array(2048, 128), array(8, 128)), [pltpu.VMEM((64, 512...  10.6 us
    unnamed x34, local copies, waits for them, and re-layouts  6.52 us
    mul x2, local copies, waits for them, and re-layouts, spread_rows(): return (padded[:, None, :, None] * eye[None, :, None, :]).reshape(64, 512)  3.7 us
  transfers between devices with their start and end apart: 3, of which 3 were waited for; matrix products, arithmetic and copies ran while one was open for 8% of the time, Pallas kernels for 0%

profile of v1, /device:TPU:8, one launch (start us, length us, event | category | flops | bytes accessed | tf_op | source)
XLA Modules:
  0.0 173.0 jit_solution(14706127476375255200)
XLA Ops:
  0.7 0.8 slice_reduce_fusion.1
  1.5 0.1 stack_tile.12
  1.7 0.1 tile.43
  1.8 0.1 stack_tile.15
  1.9 0.1 copy.15
  2.0 0.1 reshape.105
  2.2 0.1 tile.41
  2.3 0.1 stack_tile.14
  2.5 0.1 tile.39
  2.6 0.1 stack_tile.13
  2.7 0.9 copy-done.3
  3.6 0.6 input_depth.1
  4.3 17.3 %all_to_all.35 = f32[16,16,128]{2,1,0:T(8,128)S(1)} all-to-all(f32[16,16,128]{2,1,0:T(8,128)S(1)} %bitcast.39), channel_id=1, replica_groups=mesh['seed'=2,'px'=16,'py'=8] {'px'}, dimensions={0} | all-to-all | bytes 262144 | tf_op jit(solution)/shard_map/all_to_all | solution.py:266
  21.6 1.0 input_rows.1
  22.5 6.0 %all-to-all-start.1 = ((f32[8,8,128]{2,1,0:T(8,128)}), f32[8,8,128]{2,1,0:T(8,128)S(1)}, u32[]{:S(2)}, u32[]{:S(2)}) async-start(f32[8,8,128]{2,1,0:T(8,128)} %bitcast.6), calls=%async_computation.1 | async-start | bytes 65536 | tf_op jit(solution)/shard_map/all_to_all | solution.py:266
  28.5 0.8 broadcast_in_dim.30
  29.3 0.1 reshape.110
  29.4 2.7 %reshape.111.weight_ref = f32[2,4,64,1024]{3,2,1,0:T(8,128)S(1)} reshape(f32[2,4,32,2,1024]{4,3,2,1,0:T(2,128)} %param.14) | data formatting | bytes 4194304 | tf_op jit(solution)/shard_map/reshape | solution.py:304
  32.1 4.1 %all-to-all-done.1 = f32[8,8,128]{2,1,0:T(8,128)S(1)} async-done(((f32[8,8,128]{2,1,0:T(8,128)}), f32[8,8,128]{2,1,0:T(8,128)S(1)}, u32[]{:S(2)}, u32[]{:S(2)}) %all-to-all-start.1) | async-done | bytes 32800 | tf_op jit(solution)/shard_map/all_to_all | solution.py:266
  36.3 2.4 %mix.1 = (f32[32,128]{1,0:T(8,128)S(1)}, f32[8,4,8,128]{3,2,1,0:T(8,128)S(1)}) custom-call(s32[8,128]{1,0:T(8,128)S(1)} %stack.2.freq_ref, f32[64,128]{1,0:T(8,128)S(1)} %bitcast.41, f32[8,1024]{1,0:T(8,128)S(1)} %pad.15.lift_ref, f32[2,4,64,1024]{3,2,1,0:T(8,128)S(1)} %reshape.111.weight_ref), custom_call_target="tpu_custom_call" | custom-call | tf_op jit(solution)/shard_map/mix/pallas_call | solution.py:315
  38.8 10.9 %all_to_all.36 = f32[8,4,8,128]{3,2,1,0:T(8,128)S(1)} all-to-all(f32[8,4,8,128]{3,2,1,0:T(8,128)S(1)} %get-tuple-element.10), channel_id=1, replica_groups=mesh['seed'=2,'px'=16,'py'=8] {'py'}, dimensions={0} | all-to-all | bytes 262144 | tf_op jit(solution)/shard_map/all_to_all | solution.py:266
  49.7 1.4 expand.1
  51.1 1.0 copy-done.1
  52.0 7.2 %all-to-all-start.3 = ((f32[128,16,128]{2,1,0:T(8,128)}), f32[128,16,128]{2,1,0:T(8,128)S(1)}, u32[]{:S(2)}, u32[]{:S(2)}) async-start(f32[128,16,128]{2,1,0:T(8,128)} %bitcast.31), calls=%async_computation.3 | async-start | bytes 2097152 | tf_op jit(solution)/shard_map/all_to_all | solution.py:266
  59.3 0.1 fusion.5
  59.4 0.7 tile.46.mask_ref
  60.1 1.6 broadcast_multiply_fusion
  61.8 1.9 %mul.67 = f32[64,512]{1,0:T(8,128)S(1)} reshape(f32[4,16,32,16]{3,2,1,0:T(8,128)} %get-tuple-element.18) | data formatting | bytes 262144 | tf_op jit(solution)/shard_map/mul | solution.py:272
  63.6 1.9 %mul.64.point_ref = f32[64,512]{1,0:T(8,128)S(1)} reshape(f32[4,16,32,16]{3,2,1,0:T(8,128)} %get-tuple-element.19) | data formatting | bytes 262144 | tf_op jit(solution)/shard_map/mul | solution.py:272
  65.5 19.8 %all-to-all-done.3 = f32[128,16,128]{2,1,0:T(8,128)S(1)} async-done(((f32[128,16,128]{2,1,0:T(8,128)}), f32[128,16,128]{2,1,0:T(8,128)S(1)}, u32[]{:S(2)}, u32[]{:S(2)}) %all-to-all-start.3) | async-done | bytes 1048608 | tf_op jit(solution)/shard_map/all_to_all | solution.py:266
  85.3 0.9 copy-done.4
  86.2 0.7 copy-done.8
  86.9 0.9 copy-done.9
  87.8 0.7 copy-done.12
  88.5 10.6 %grid.1 = (f32[2048,128]{1,0:T(8,128)S(1)}, f32[8,128]{1,0:T(8,128)S(1)}) custom-call(s32[8,128]{1,0:T(8,128)S(1)} %copy-done.8, f32[2048,128]{1,0:T(8,128)S(1)} %bitcast.30, f32[3,8,16,128]{3,2,1,0:T(8,128)S(1)} %bitcast.35, f32[3,8,16,128]{3,2,1,0:T(8,128)S(1)} %bitcast.40, f32[8,128]{1,0:T(8,128)S(1)} %copy-done.12, f32[64,512]{1,0:T(8,128)S(1)} %mul.64.point_ref, ...), custom_call_target="tpu_custom_call" | custom-call | tf_op jit(solution)/shard_map/grid/pallas_call | solution.py:326
  99.1 32.8 %all_to_all.37 = f32[128,16,128]{2,1,0:T(8,128)S(1)} all-to-all(f32[128,16,128]{2,1,0:T(8,128)S(1)} %bitcast.33), channel_id=1, replica_groups=mesh['seed'=2,'px'=16,'py'=8] {'py','px'}, dimensions={0} | all-to-all | bytes 2097152 | tf_op jit(solution)/shard_map/all_to_all | solution.py:266
  131.9 1.1 reduce.9
  133.1 12.4 %all_to_all.38.pieces_ref = f32[8,4,8,128]{3,2,1,0:T(8,128)S(1)} all-to-all(f32[8,4,8,128]{3,2,1,0:T(8,128)S(1)} %bitcast.36), channel_id=1, replica_groups=mesh['seed'=2,'px'=16,'py'=8] {'py'}, dimensions={0} | all-to-all | bytes 262144 | tf_op jit(solution)/shard_map/all_to_all | solution.py:266
  145.5 3.1 %back.1 = (f32[2,4,64,1024]{3,2,1,0:T(8,128)S(1)}, f32[8,128]{1,0:T(8,128)S(1)}) custom-call(f32[8,4,8,128]{3,2,1,0:T(8,128)S(1)} %all_to_all.38.pieces_ref, f32[32,128]{1,0:T(8,128)S(1)} %copy-done.11, f32[8,1024]{1,0:T(8,128)S(1)} %copy-done.6, f32[2,4,64,1024]{3,2,1,0:T(8,128)S(1)} %reshape.111.weight_ref, f32[8,128]{1,0:T(8,128)S(1)} %get-tuple-element.13.small_ref), custom_call_target="tpu_custom_call" | custom-call | tf_op jit(solution)/shard_map/back/pallas_call | solution.py:337
  148.6 1.4 copy-done.2
  149.9 0.7 broadcast_in_dim.31
  150.6 7.2 %all-to-all-start.6 = ((f32[128,3,128]{2,1,0:T(4,128)}), f32[128,3,128]{2,1,0:T(4,128)S(1)}, u32[]{:S(2)}, u32[]{:S(2)}) async-start(f32[128,3,128]{2,1,0:T(4,128)} %broadcast_in_dim.31), calls=%async_computation.6 | async-start | bytes 524288 | tf_op jit(solution)/shard_map/all_to_all | solution.py:266
  157.9 3.4 %reshape.118 = f32[2,4,32,2,1024]{4,3,2,1,0:T(2,128)} reshape(f32[2,4,64,1024]{3,2,1,0:T(8,128)} %copy-done.2) | data formatting | bytes 4194304 | tf_op jit(solution)/shard_map/reshape | solution.py:350
  161.3 9.3 %all-to-all-done.6 = f32[128,3,128]{2,1,0:T(4,128)S(1)} async-done(((f32[128,3,128]{2,1,0:T(4,128)}), f32[128,3,128]{2,1,0:T(4,128)S(1)}, u32[]{:S(2)}, u32[]{:S(2)}) %all-to-all-start.6) | async-done | bytes 196640 | tf_op jit(solution)/shard_map/all_to_all | solution.py:266
  170.7 0.1 reduce_sum.9
  170.8 0.7 fusion.1
  171.5 0.6 slice_multiply_fusion
  172.2 0.8 convolution_multiply_fusion
  (47 shorter events, 0.5 us)
Async XLA Ops:
  0.6 58.6 %copy-start = (f32[32,32]{1,0:T(8,128)S(1)}, f32[32,32]{1,0:T(8,128)}, u32[]{:S(2)}) copy-start(f32[32,32]{1,0:T(8,128)} %param.13) | copy-start | bytes 12292
  2.7 47.0 %copy-start.7 = (s32[8,128]{1,0:T(8,128)}, s32[8,128]{1,0:T(8,128)S(1)}, u32[]{:S(2)}) copy-start(s32[8,128]{1,0:T(8,128)S(1)} %stack.2.freq_ref) | copy-start | bytes 12292
  2.7 0.9 copy-start.3
  22.5 13.7 %all-to-all-start.1 = ((f32[8,8,128]{2,1,0:T(8,128)}), f32[8,8,128]{2,1,0:T(8,128)S(1)}, u32[]{:S(2)}, u32[]{:S(2)}) async-start(f32[8,8,128]{2,1,0:T(8,128)} %bitcast.6), calls=%async_computation.1 | async-start | bytes 65536 | tf_op jit(solution)/shard_map/all_to_all | solution.py:266
  32.1 19.9 %copy-start.5 = (f32[8,1024]{1,0:T(8,128)}, f32[8,1024]{1,0:T(8,128)S(1)}, u32[]{:S(2)}) copy-start(f32[8,1024]{1,0:T(8,128)S(1)} %pad.15.lift_ref) | copy-start | bytes 98308
  38.7 11.0 %copy-start.10 = (f32[32,128]{1,0:T(8,128)}, f32[32,128]{1,0:T(8,128)S(1)}, u32[]{:S(2)}) copy-start(f32[32,128]{1,0:T(8,128)S(1)} %get-tuple-element.12.modes_ref) | copy-start | bytes 49156
  38.7 20.5 %copy-start.16 = (f32[3,32]{1,0:T(4,128)S(1)}, f32[3,32]{1,0:T(4,128)}, u32[]{:S(2)}) copy-start(f32[3,32]{1,0:T(4,128)} %param.15) | copy-start | bytes 1156
  38.7 20.6 %copy-start.13 = (f32[32,3]{0,1:T(4,128)S(1)}, f32[32,3]{0,1:T(4,128)}, u32[]{:S(2)}) copy-start(f32[32,3]{0,1:T(4,128)} %param.12) | copy-start | bytes 1156
  38.7 20.7 %copy-start.15 = (s32[8,16]{1,0:T(8,128)S(1)}, s32[8,16]{1,0:T(8,128)}, u32[]{:S(2)}) copy-start(s32[8,16]{1,0:T(8,128)} %param.10) | copy-start | bytes 1540
  51.0 1.0 copy-start.1
  52.0 33.3 %all-to-all-start.3 = ((f32[128,16,128]{2,1,0:T(8,128)}), f32[128,16,128]{2,1,0:T(8,128)S(1)}, u32[]{:S(2)}, u32[]{:S(2)}) async-start(f32[128,16,128]{2,1,0:T(8,128)} %bitcast.31), calls=%async_computation.3 | async-start | bytes 2097152 | tf_op jit(solution)/shard_map/all_to_all | solution.py:266
  85.3 0.9 copy-start.4
  86.2 0.7 copy-start.8
  86.9 0.9 copy-start.9
  87.8 0.7 copy-start.12
  99.1 46.4 %copy-start.6 = (f32[8,1024]{1,0:T(8,128)S(1)}, f32[8,1024]{1,0:T(8,128)}, u32[]{:S(2)}) copy-start(f32[8,1024]{1,0:T(8,128)} %copy-done.5) | copy-start | bytes 98308
  99.1 46.4 %copy-start.11 = (f32[32,128]{1,0:T(8,128)S(1)}, f32[32,128]{1,0:T(8,128)}, u32[]{:S(2)}) copy-start(f32[32,128]{1,0:T(8,128)} %copy-done.10) | copy-start | bytes 49156
  148.6 1.4 copy-start.2
  150.6 20.0 %all-to-all-start.6 = ((f32[128,3,128]{2,1,0:T(4,128)}), f32[128,3,128]{2,1,0:T(4,128)S(1)}, u32[]{:S(2)}, u32[]{:S(2)}) async-start(f32[128,3,128]{2,1,0:T(4,128)} %broadcast_in_dim.31), calls=%async_computation.6 | async-start | bytes 524288 | tf_op jit(solution)/shard_map/all_to_all | solution.py:266
  157.9 14.3 %copy-start.14 = (f32[32,3]{0,1:T(4,128)S(1)}, f32[32,3]{0,1:T(4,128)}, u32[]{:S(2)}) copy-start(f32[32,3]{0,1:T(4,128)} %param.12) | copy-start | bytes 1156

commit v2 on v1

v2 whole, which is shorter than its diff:
```python
import math

import jax
import jax.numpy as jnp
from jax import lax
from jax.experimental import pallas as pl
from jax.experimental.pallas import tpu as pltpu
from jax.sharding import PartitionSpec as P

C = 32
N = 128
M = 32
F32 = jnp.float32
BF16 = jnp.bfloat16
SCALE = 1.0 / float(N**3)
GELU_A = math.sqrt(2.0 / math.pi)
GELU_B = 0.044715

NN = (((1,), (0,)), ((), ()))
NT = (((1,), (1,)), ((), ()))


def split(value):
    high = value.astype(BF16)
    return high, (value - high.astype(F32)).astype(BF16)


def mul(left, right, dims):
    return lax.dot_general(left, right, dims, preferred_element_type=F32)


def dot3(left, right, dims=NN):
    left_high, left_low = left if isinstance(left, tuple) else split(left)
    right_high, right_low = right if isinstance(right, tuple) else split(right)
    return (
        mul(left_low, right_high, dims)
        + mul(left_high, right_low, dims)
        + mul(left_high, right_high, dims)
    )


def iota(shape, axis):
    return lax.broadcasted_iota(jnp.int32, shape, axis)


def wave(turns):
    place = jnp.abs((turns & (N - 1)) - N // 2).astype(F32)
    angle = (place - N / 4) * (2.0 * math.pi / N)
    square = angle * angle
    series = 1.0 / 39916800.0
    for term in (362880.0, 5040.0, 120.0, 6.0, 1.0):
        series = 1.0 / term - square * series
    return angle * series


def dot2k(left, right):
    left_high, left_low = split(left)
    right_high, right_low = right if isinstance(right, tuple) else split(right)
    wide = jnp.concatenate([left_high, left_low], axis=1)
    tall = jnp.concatenate([right_high, right_high], axis=0)
    return mul(left_high, right_low, NN) + mul(wide, tall, NN)


def frequency_rows(modes):
    place = iota((M, 128), 1)
    slot = iota((M, 128), 0)
    modes = modes.astype(F32).astype(BF16)
    orders = (
        (0, place % 32),
        (1, place % 32),
        (2, 2 * (place // 2 % 16) + place // 32 % 2),
        (0, 4 * (place // 8 % 8) + place % 4),
    )
    rows = []
    for dim, order in orders:
        pick = jnp.where(slot == order, 1.0, 0.0).astype(BF16)
        rows.append(mul(modes, pick, NN)[dim : dim + 1])
    return jnp.concatenate(rows + rows, axis=0).astype(jnp.int32)


def regroup(pieces):
    group = iota(pieces[0].shape, 1) // 16
    out = []
    for target in range(8):
        total = pieces[target]
        for source in range(8):
            if source != target:
                moved = pltpu.roll(pieces[source], (16 * (source - target)) % 128, 1)
                total = jnp.where(group == source, moved, total)
        out.append(total)
    return out


def depth_waves(freq):
    shape = (N, 128)
    return wave(iota(shape, 0) * freq + 32 * (iota(shape, 1) & 1))


def input_depth(modes_ref, field_ref, freq_ref, out_ref):
    freq = frequency_rows(modes_ref[...])
    freq_ref[...] = freq
    table = split(depth_waves(freq[2:3]).T[:64])
    lane = iota((32, 128), 1)
    blank = jnp.zeros((16, N), F32)
    for x in range(8):
        rows = [field_ref[channel, x] for channel in range(3)] + [blank]
        both = jnp.concatenate(rows + rows, axis=0)
        result = dot3(table, both, NT)
        out_ref[pl.ds(x, 32, stride=8), :] = jnp.where(lane < 64, result[:32], result[32:])


def rows_waves(freq_row, phase):
    shape = (256, 128)
    row = iota(shape, 0)
    place = (row // 16) * 8 + row % 8
    return place * freq_row + phase(row // 8 % 2)


def input_rows(freq_ref, pieces_ref, out_ref):
    lane = iota((256, 128), 1)
    table = wave(rows_waves(freq_ref[3:4, :], lambda part: 32 * ((lane // 4) % 2 - part)))
    out_ref[...] = dot3(table.T[:64], pieces_ref[...])


def weight_rows(weight_ref, part, p):
    base = 512 * (4 * part + p)
    return jnp.concatenate(
        [
            jnp.concatenate(
                [weight_ref[pl.ds(base + 2 * k + r, 32, stride=16), :] for k in range(8)], axis=1
            )
            for r in range(2)
        ],
        axis=0,
    )


def lift_spread(lift_ref):
    pick = jnp.where(iota((32, 1024), 0) == iota((32, 1024), 1) // 32, 1.0, 0.0).astype(BF16)
    high, low = split(lift_ref[...])
    return mul(low, pick, NN) + mul(high, pick, NN)


def spread_modes(modes, lift):
    turned = modes.T
    total = turned[:, 0:1] * lift[0:1]
    for channel in (1, 2):
        total = total + turned[:, channel : channel + 1] * lift[channel : channel + 1]
    return total


def fold_table():
    return jnp.where(iota((32, 1024), 0) == iota((32, 1024), 1) % 32, SCALE, 0.0).astype(BF16)


def mix_kernel(freq_ref, pieces_ref, lift_ref, weight_ref, held_modes_ref, out_ref, held_ref):
    pieces = [pieces_ref[8 * source : 8 * source + 8, :] for source in range(8)]
    rows = split(jnp.concatenate(regroup(pieces), axis=0))
    shape = (N, 128)
    lane = iota(shape, 1)
    turns = iota(shape, 0) * freq_ref[1:2, :]
    held_ref[:, :128] = dot3(rows, wave(turns + 32 * (lane // 64)))
    held_ref[:, 128:] = dot3(rows, wave(turns + 32 * (lane // 64) - 32))
    first_slot = iota((4, 128), 1) // 32 % 2 == 0
    held_modes_ref[...] = jnp.zeros((32, 128), F32)
    for channel in range(3):
        both = []
        for parity in range(2):
            base = 8 * (4 * parity + channel)
            both.append(held_ref[base : base + 4, :128] + held_ref[base + 4 : base + 8, 128:])
        held_modes_ref[pl.ds(channel, 4, stride=8), :] = jnp.where(first_slot, both[0], both[1])
    lift = lift_spread(lift_ref)
    fold = fold_table()
    for p in range(4):
        spread = spread_modes(held_modes_ref[8 * p : 8 * p + 8, :], lift)
        real, imag = spread[:64], spread[64:]
        first, second = weight_rows(weight_ref, 0, p), weight_rows(weight_ref, 1, p)
        product = jnp.concatenate([first * real - second * imag, second * real + first * imag], axis=0)
        high, low = split(product)
        mixed = mul(fold, low, NT) + mul(fold, high, NT)
        for target in range(8):
            start = 8 * (target // 2)
            out_ref[target, p] = mixed[start : start + 8]


def plane_waves(freq_ref):
    shape = (256, 128)
    row, lane = iota(shape, 0), iota(shape, 1)
    table = wave((row % 128) * freq_ref[1:2, :] + 32 * (lane // 64 - row // 128))
    parity = lax.axis_index("py") % 2
    return split(jnp.where(lane // 32 % 2 == parity, table, 0.0))


def expand(freq_ref, pieces_ref, out_ref, mark_ref, held_ref):
    result = dot3(pieces_ref[...], plane_waves(freq_ref), NT)
    held_ref[:256, :] = result[:, :128]
    held_ref[256:, :] = result[:, 128:]
    parts = []
    for part in range(2):
        parts.append(
            regroup([held_ref[pl.ds(256 * part + o, 32, stride=8), :] for o in range(8)])
        )
    lane = iota((256, 128), 1)
    table = split(wave(rows_waves(freq_ref[0:1, :], lambda part: 32 * (lane // 32 - part)))[:, :64])
    for pair in range(4):
        wide = jnp.concatenate(
            [
                jnp.concatenate([parts[part][2 * pair + k] for part in range(2)], axis=0)
                for k in range(2)
            ],
            axis=1,
        )
        result = dot3(table, wide)
        for k in range(2):
            start = 256 * (2 * pair + k)
            out_ref[start : start + 256, :] = result[:, 128 * k : 128 * k + 128]
    mark_ref[...] = jnp.zeros((8, 128), F32)


def tables_kernel(mark_ref, mask_ref, lift_ref, mix_ref, proj_ref, point_out, proj_out, mask_out):
    pick = jnp.where(iota((32, 512), 0) == iota((32, 512), 1) // 16, 1.0, 0.0).astype(BF16)
    same = iota((64, 512), 0) % 16 == iota((64, 512), 1) % 16
    rows = jnp.where(iota((64, 8), 0) // 16 == iota((64, 8), 1), 1.0, 0.0).astype(BF16)

    def spread(matrix):
        high, low = split(matrix)
        wide = split(mul(high, pick, NN) + mul(low, pick, NN))
        return jnp.where(same, mul(rows, wide[0], NN) + mul(rows, wide[1], NN), 0.0)

    point_out[...] = spread(dot3(lift_ref[...], mix_ref[...], NT))
    table = spread(proj_ref[...])
    proj_out[:64] = table
    proj_out[64:] = table
    repeat = jnp.where(iota((16, 128), 0) == iota((16, 128), 1) % 16, 2.0, 0.0).astype(BF16)
    mask = mul(mask_ref[...].astype(F32).astype(BF16), repeat, NN)
    mask_out[...] = mask + 0.0 * mark_ref[...]


def grid_kernel(
    freq_ref, pieces_ref, field_ref, target_ref, mask_ref, point_ref, proj_ref,
    out_ref, point_grad, proj_grad,
):
    waves = depth_waves(freq_ref[2:3, :]).T[:64]
    point = point_ref[...]
    proj = split(proj_ref[...])
    back = jnp.concatenate(
        [proj[0], proj[1][:64], jnp.zeros((64, 512), BF16)], axis=0
    )
    lower = iota((N, 128), 1) < 64
    blank = jnp.zeros((16, N), F32)
    point_grad[...] = jnp.zeros_like(point_grad)
    proj_grad[...] = jnp.zeros_like(proj_grad)

    def plane(x, carry):
        rows = [field_ref[channel, x] for channel in range(3)] + [blank]
        stack = jnp.concatenate([waves] + rows, axis=0)
        aims = [target_ref[channel, x] for channel in range(3)] + [blank]
        aim = jnp.concatenate(aims + aims, axis=0).T
        coefs = [pieces_ref[pl.ds(512 * o + x, 64, stride=8), :] for o in range(4)]
        coefs = jnp.concatenate([jnp.concatenate(coefs, axis=1), point], axis=0)
        preact = dot2k(stack.T, coefs)
        cube = preact * preact
        bend = jnp.tanh(preact * (GELU_A + (GELU_A * GELU_B) * cube))
        half = 0.5 + 0.5 * bend
        active = split(preact * half)
        slope = half + preact * (0.5 - 0.5 * bend * bend) * (
            GELU_A + (3.0 * GELU_A * GELU_B) * cube
        )
        error = mask_ref[pl.ds(x, 1), :] * (dot3(active, proj, NT) - aim)
        high = error.astype(BF16)
        both = jnp.where(lower, high.astype(F32), error - high.astype(F32)).astype(BF16)
        rate = mul(jnp.concatenate([both, high], axis=1), back, NN) * slope
        both = dot2k(stack, rate)
        for o in range(4):
            out_ref[pl.ds(512 * o + x, 64, stride=8), :] = both[:64, 128 * o : 128 * o + 128]
        point_grad[...] += both[64:]
        proj_grad[...] += dot2k(error.T[:64], active)
        return carry

    lax.fori_loop(0, 8, plane, 0)


def pick_kernel(point_grad, proj_grad, small_ref):
    same = iota((64, 512), 0) % 16 == iota((64, 512), 1) % 16
    pick = jnp.where(iota((8, 64), 0) == iota((8, 64), 1) // 16, 1.0, 0.0)
    total = jnp.zeros((8, 128), F32)
    for offset, ref in ((0, point_grad), (32, proj_grad)):
        kept = dot3(pick, jnp.where(same, ref[...], 0.0))
        place = jnp.where(iota((512, 128), 0) // 16 + offset == iota((512, 128), 1), 1.0, 0.0)
        total = total + dot3(kept, place)
    small_ref[...] = total


def reduce_kernel(freq_ref, pieces_ref, out_ref, held_ref):
    lane = iota((256, 128), 1)
    table = wave(rows_waves(freq_ref[0:1, :], lambda part: 32 * ((lane // 32) % 2 - part)))
    table = split(table.T[:64])
    results = []
    for j in range(8):
        results.append(dot3(table, pieces_ref[256 * j : 256 * j + 256, :]))
    for part in range(2):
        pieces = regroup([result[32 * part : 32 * part + 32] for result in results])
        for o in range(8):
            held_ref[pl.ds(256 * part + o, 32, stride=8), :] = pieces[o]
    rows = jnp.concatenate([held_ref[:256, :], held_ref[256:, :]], axis=1)
    out_ref[...] = dot3(rows, plane_waves(freq_ref))


def outer_grads(pieces_ref, tile, p):
    grads = jnp.concatenate(
        [pieces_ref[2 * o, p] + pieces_ref[2 * o + 1, p] for o in range(4)], axis=0
    )
    return mul(jnp.concatenate(split(grads.T), axis=1), tile, NN)


def lift_kernel(pieces_ref, held_modes_ref, weight_ref, small_ref, sum_ref):
    tile = fold_table()
    tile = jnp.concatenate([tile, tile], axis=0)
    total = [jnp.zeros((1, 1024), F32)] * 3
    for p in range(4):
        outer = outer_grads(pieces_ref, tile, p)
        real, imag = outer[:64], outer[64:]
        first, second = weight_rows(weight_ref, 0, p), weight_rows(weight_ref, 1, p)
        back = jnp.concatenate([first * real + second * imag, first * imag - second * real], axis=0)
        turned = held_modes_ref[8 * p : 8 * p + 8, :].T
        for channel in range(3):
            product = turned[:, channel : channel + 1] * back
            total[channel] = total[channel] + jnp.sum(product, axis=0, keepdims=True)
    total = jnp.concatenate(total + [jnp.zeros((5, 1024), F32)], axis=0)
    place = jnp.where(iota((1024, 128), 0) // 32 + 64 == iota((1024, 128), 1), 1.0, 0.0)
    total = small_ref[...] + dot3(total, place)
    total = jnp.where(iota((8, 128), 0) < 4, total, pltpu.roll(total, 4, 0))
    for target in range(64):
        sum_ref[8 * target : 8 * target + 8, :] = total


def grad_kernel(pieces_ref, held_modes_ref, lift_ref, grad_ref):
    lift = lift_spread(lift_ref)
    tile = fold_table()
    tile = jnp.concatenate([tile, tile], axis=0)
    for p in range(4):
        spread = spread_modes(held_modes_ref[8 * p : 8 * p + 8, :], lift)
        outer = outer_grads(pieces_ref, tile, p)
        real, imag = spread[:64], spread[64:]
        grad_real, grad_imag = outer[:64], outer[64:]
        results = (real * grad_real + imag * grad_imag, real * grad_imag - imag * grad_real)
        for part in range(2):
            base = 512 * (4 * part + p)
            for r in range(2):
                for k in range(8):
                    grad_ref[pl.ds(base + 2 * k + r, 32, stride=16), :] = results[part][
                        32 * r : 32 * r + 32, 128 * k : 128 * k + 128
                    ]


def last_kernel(sum_ref, lift_ref, mix_ref, lift_out, mix_out, proj_out):
    total = jnp.concatenate([sum_ref[...], jnp.zeros((124, 128), F32)], axis=0) * SCALE
    cross = total[:8, :32]
    mix_out[...] = dot3(total.T[:32, :8], lift_ref[...])
    lift_out[...] = (dot3(cross, mix_ref[...]) + total[:8, 64:96])[:3]
    proj_out[...] = total[:3, 32:64]


def call(kernel, shapes, scratch=(), name=None):
    return pl.pallas_call(
        kernel,
        out_shape=shapes,
        scratch_shapes=list(scratch),
        name=name,
        compiler_params=pltpu.CompilerParams(vmem_limit_bytes=48 * 1024 * 1024),
    )


def array(*shape):
    return jax.ShapeDtypeStruct(shape, F32)


def exchange(value, axes):
    return lax.all_to_all(value, axes, split_axis=0, concat_axis=0, tiled=True)


def body(
    input_field,
    target_field,
    row_mask,
    modes,
    lift_weight,
    mix_weight,
    spectral_weight,
    proj_weight,
):
    field = input_field[0]
    target = target_field[0]
    weight = spectral_weight.reshape(2, 4, 32, 2, 8, 128).transpose(0, 1, 2, 4, 3, 5)
    weight = weight.reshape(4096, 128)
    lift_rows = jnp.pad(lift_weight.T, ((0, 5), (0, 0)))
    proj_rows = jnp.pad(proj_weight, ((0, 5), (0, 0)))

    freq, pieces = call(
        input_depth,
        (jax.ShapeDtypeStruct((8, 128), jnp.int32), array(256, 128)),
        name="input_depth",
    )(modes, field)
    pieces = exchange(pieces.reshape(16, 16, 128), "px").reshape(256, 128)
    pieces = call(input_rows, array(64, 128), name="input_rows")(freq, pieces)
    pieces = exchange(pieces.reshape(8, 8, 128), "py").reshape(64, 128)
    held_modes, pieces = call(
        mix_kernel,
        (array(32, 128), array(8, 4, 8, 128)),
        [pltpu.VMEM((64, 256), F32)],
        name="mix",
    )(freq, pieces, lift_rows, weight)
    pieces = exchange(pieces, "py").reshape(256, 128)
    pieces, mark = call(
        expand,
        (array(2048, 128), array(8, 128)),
        [pltpu.VMEM((512, 128), F32)],
        name="expand",
    )(freq, pieces)
    point, proj, mask = call(
        tables_kernel, (array(64, 512), array(128, 512), array(8, 128)), name="tables"
    )(mark, row_mask, lift_rows, mix_weight, proj_rows)
    pieces = exchange(pieces.reshape(128, 16, 128), ("py", "px")).reshape(2048, 128)
    pieces, point_grad, proj_grad = call(
        grid_kernel, (array(2048, 128), array(64, 512), array(64, 512)), name="grid"
    )(freq, pieces, field, target, mask, point, proj)
    small = call(pick_kernel, array(8, 128), name="pick")(point_grad, proj_grad)
    pieces = exchange(pieces.reshape(128, 16, 128), ("py", "px")).reshape(2048, 128)
    pieces = call(reduce_kernel, array(256, 128), [pltpu.VMEM((512, 128), F32)], name="reduce")(
        freq, pieces
    )
    pieces = exchange(pieces.reshape(8, 4, 8, 128), "py")
    sums = call(lift_kernel, array(512, 128), name="lift")(pieces, held_modes, weight, small)
    grad = call(grad_kernel, array(4096, 128), name="grad")(pieces, held_modes, lift_rows)
    sums = exchange(sums.reshape(128, 4, 128), ("px", "py"))
    sums = jnp.sum(sums, axis=0)
    lift_total, mix_total, proj_total = call(
        last_kernel, (array(3, 32), array(32, 32), array(3, 32)), name="last"
    )(sums, lift_rows, mix_weight)
    grad = grad.reshape(2, 4, 32, 8, 2, 128).transpose(0, 1, 2, 4, 3, 5)
    return lift_total.T, mix_total, proj_total, grad.reshape(spectral_weight.shape)


def solution(mesh):
    in_specs = (
        P(None, None, "px", "py", None),
        P(None, None, "px", "py", None),
        P(("seed", "px"), "py"),
        P("seed", None),
        P("seed", None),
        P("seed", None),
        P("seed", "py", None, "px", None),
        P("seed", None),
    )
    out_specs = (
        P("seed", None),
        P("seed", None),
        P("seed", None),
        P("seed", "py", None, "px", None),
    )
    return jax.shard_map(body, mesh=mesh, in_specs=in_specs, out_specs=out_specs, check_vma=False)
```

time: 174 us -> 165 us (0.948)
  local copies, waits for them, and re-layouts: 20.6 us -> 3.91 us
  waiting for transfers between devices: 33.3 us -> 49.1 us
  blocking collectives: 73.4 us -> 60 us
  starting transfers between devices: 20.4 us -> 25.8 us
  Pallas kernels: 20.2 us -> 24.5 us
  other arithmetic: 2.45 us -> 0.14 us
    all_to_all x3 -> x4, waiting for transfers between devices: 33.3 us -> 49.1 us  [exchange(): return lax.all_to_all(value, axes, split_axis=0, concat_axis=0, tiled=True)]
    all_to_all x4 -> x3, blocking collectives: 73.4 us -> 60 us  [exchange(): return lax.all_to_all(value, axes, split_axis=0, concat_axis=0, tiled=True)]
    reshape x4 -> x0, local copies, waits for them, and re-layouts: 6.32 us -> none  [the longest x1 3.45 us: body(): grad.reshape(spectral_weight.shape)]
    all_to_all x3 -> x4, starting transfers between devices: 20.4 us -> 25.8 us  [exchange(): return lax.all_to_all(value, axes, split_axis=0, concat_axis=0, tiled=True)]
    pallas_call x4 -> x8, Pallas kernels: 15.7 us -> 19.7 us  [the longest x1 8.73 us: body(): call(grid_kernel, (array(2048, 128), array(64, 512), array(64, 512)), nam...]
    mul x2 -> x0, local copies, waits for them, and re-layouts: 3.7 us -> none  [spread_rows(): return (padded[:, None, :, None] * eye[None, :, None, :]).reshape(64, 512)]
    unnamed x34 -> x18, local copies, waits for them, and re-layouts: 6.52 us -> 3.22 us
    mul x3 -> x0, other arithmetic: 2.29 us -> none  [the longest x1 1.64 us: spread_rows(): return (padded[:, None, :, None] * eye[None, :, None, :]).reshape(64, 512)]
  transfers between devices with their start and end apart: 3 -> 4, of which waited for: 3 -> 4; matrix products, arithmetic and copies ran while one was open for 8% -> 0% of each run, Pallas kernels for 0% -> 3%
where the time goes in v2:
time: 165 us; the launch traced here: 164 us
  blocking collectives  60 us (36%)
  waiting for transfers between devices  49.1 us (30%)
  starting transfers between devices  25.8 us (16%)
  Pallas kernels  24.5 us (15%)
  local copies, waits for them, and re-layouts  3.91 us (2%)
    all_to_all x3, blocking collectives, exchange(): return lax.all_to_all(value, axes, split_axis=0, concat_axis=0, tiled=True)  60 us
    all_to_all x4, waiting for transfers between devices, exchange(): return lax.all_to_all(value, axes, split_axis=0, concat_axis=0, tiled=True)  49.1 us
    all_to_all x4, starting transfers between devices, exchange(): return lax.all_to_all(value, axes, split_axis=0, concat_axis=0, tiled=True)  25.8 us
    pallas_call x1, Pallas kernels, body(): call(grid_kernel, (array(2048, 128), array(64, 512), array(64, 512)), nam...  8.73 us
  transfers between devices with their start and end apart: 4, of which 4 were waited for; matrix products, arithmetic and copies ran while one was open for 0% of the time, Pallas kernels for 3%

profile of v2, /device:TPU:8, one launch (start us, length us, event | category | flops | bytes accessed | tf_op | source)
XLA Modules:
  0.0 164.2 jit_solution(1249546129599870710)
XLA Ops:
  0.6 0.0 copy-start.2
  0.6 0.9 copy-done.2
  1.6 0.0 copy-start.7
  1.6 0.7 copy-done.7
  2.2 0.8 input_depth.1
  3.0 17.3 %all_to_all.35 = f32[16,16,128]{2,1,0:T(8,128)S(1)} all-to-all(f32[16,16,128]{2,1,0:T(8,128)S(1)} %bitcast.36), channel_id=1, replica_groups=mesh['seed'=2,'px'=16,'py'=8] {'px'}, dimensions={0} | all-to-all | bytes 262144 | tf_op jit(solution)/shard_map/all_to_all | solution.py:379
  20.3 1.0 input_rows.1
  21.3 6.0 %all-to-all-start.1 = ((f32[8,8,128]{2,1,0:T(8,128)}), f32[8,8,128]{2,1,0:T(8,128)S(1)}, u32[]{:S(2)}, u32[]{:S(2)}) async-start(f32[8,8,128]{2,1,0:T(8,128)} %bitcast.3), calls=%async_computation.1 | async-start | bytes 65536 | tf_op jit(solution)/shard_map/all_to_all | solution.py:379
  27.3 0.7 pad.7.lift_ref
  28.0 7.0 %all-to-all-done.1 = f32[8,8,128]{2,1,0:T(8,128)S(1)} async-done(((f32[8,8,128]{2,1,0:T(8,128)}), f32[8,8,128]{2,1,0:T(8,128)S(1)}, u32[]{:S(2)}, u32[]{:S(2)}) %all-to-all-start.1) | async-done | bytes 32800 | tf_op jit(solution)/shard_map/all_to_all | solution.py:379
  35.0 0.0 copy-start
  35.0 1.6 copy-done
  36.6 0.0 copy-start.8
  36.6 0.0 copy-start.5
  36.6 0.0 copy-start.6
  36.6 0.0 copy-start.3
  36.6 0.0 copy-start.4
  36.6 2.1 %mix.1 = (f32[32,128]{1,0:T(8,128)S(1)}, f32[8,4,8,128]{3,2,1,0:T(8,128)S(1)}) custom-call(s32[8,128]{1,0:T(8,128)S(1)} %get-tuple-element.19.freq_ref, f32[64,128]{1,0:T(8,128)S(1)} %bitcast.35, f32[8,32]{1,0:T(8,128)S(1)} %pad.7.lift_ref, f32[4096,128]{1,0:T(8,128)S(1)} %bitcast.25), custom_call_target="tpu_custom_call" | custom-call | tf_op jit(solution)/shard_map/mix/pallas_call | solution.py:407
  38.7 10.3 %all_to_all.36 = f32[8,4,8,128]{3,2,1,0:T(8,128)S(1)} all-to-all(f32[8,4,8,128]{3,2,1,0:T(8,128)S(1)} %get-tuple-element.21), channel_id=1, replica_groups=mesh['seed'=2,'px'=16,'py'=8] {'py'}, dimensions={0} | all-to-all | bytes 262144 | tf_op jit(solution)/shard_map/all_to_all | solution.py:379
  49.0 2.3 %expand.1 = (f32[2048,128]{1,0:T(8,128)}, f32[8,128]{1,0:T(8,128)S(1)}) custom-call(s32[8,128]{1,0:T(8,128)S(1)} %get-tuple-element.19.freq_ref, f32[256,128]{1,0:T(8,128)S(1)} %bitcast.32), custom_call_target="tpu_custom_call" | custom-call | tf_op jit(solution)/shard_map/expand/pallas_call | solution.py:414
  51.3 7.2 %all-to-all-start.3 = ((f32[128,16,128]{2,1,0:T(8,128)}), f32[128,16,128]{2,1,0:T(8,128)S(1)}, u32[]{:S(2)}, u32[]{:S(2)}) async-start(f32[128,16,128]{2,1,0:T(8,128)} %bitcast.10), calls=%async_computation.3 | async-start | bytes 2097152 | tf_op jit(solution)/shard_map/all_to_all | solution.py:379
  58.5 0.0 copy-done.8
  58.6 0.0 copy-done.5
  58.6 0.0 copy-done.6
  58.6 0.6 tables.1
  59.2 24.9 %all-to-all-done.3 = f32[128,16,128]{2,1,0:T(8,128)S(1)} async-done(((f32[128,16,128]{2,1,0:T(8,128)}), f32[128,16,128]{2,1,0:T(8,128)S(1)}, u32[]{:S(2)}, u32[]{:S(2)}) %all-to-all-start.3) | async-done | bytes 1048608 | tf_op jit(solution)/shard_map/all_to_all | solution.py:379
  84.1 0.0 copy-done.3
  84.1 0.0 copy-done.4
  84.1 8.7 %grid.1 = (f32[2048,128]{1,0:T(8,128)S(1)}, f32[64,512]{1,0:T(8,128)S(1)}, f32[64,512]{1,0:T(8,128)S(1)}) custom-call(s32[8,128]{1,0:T(8,128)S(1)} %get-tuple-element.19.freq_ref, f32[2048,128]{1,0:T(8,128)S(1)} %bitcast.27, f32[3,8,16,128]{3,2,1,0:T(8,128)S(1)} %bitcast.31, f32[3,8,16,128]{3,2,1,0:T(8,128)S(1)} %bitcast.34, ...), custom_call_target="tpu_custom_call" | custom-call | tf_op jit(solution)/shard_map/grid/pallas_call | solution.py:424
  92.9 0.0 copy-start.1
  92.9 32.4 %all_to_all.37 = f32[128,16,128]{2,1,0:T(8,128)S(1)} all-to-all(f32[128,16,128]{2,1,0:T(8,128)S(1)} %bitcast.29), channel_id=1, replica_groups=mesh['seed'=2,'px'=16,'py'=8] {'py','px'}, dimensions={0} | all-to-all | bytes 2097152 | tf_op jit(solution)/shard_map/all_to_all | solution.py:379
  125.2 1.8 %reduce.1 = f32[256,128]{1,0:T(8,128)} custom-call(s32[8,128]{1,0:T(8,128)S(1)} %get-tuple-element.19.freq_ref, f32[2048,128]{1,0:T(8,128)S(1)} %bitcast.28), custom_call_target="tpu_custom_call" | custom-call | tf_op jit(solution)/shard_map/reduce/pallas_call | solution.py:429
  127.0 4.6 %all-to-all-start.5 = ((f32[8,4,8,128]{3,2,1,0:T(8,128)}), f32[8,4,8,128]{3,2,1,0:T(8,128)S(1)}, u32[]{:S(2)}, u32[]{:S(2)}) async-start(f32[8,4,8,128]{3,2,1,0:T(8,128)} %bitcast.15), calls=%async_computation.5 | async-start | bytes 262144 | tf_op jit(solution)/shard_map/all_to_all | solution.py:379
  131.7 0.5 pick.1.small_ref
  132.2 7.4 %all-to-all-done.5.pieces_ref = f32[8,4,8,128]{3,2,1,0:T(8,128)S(1)} async-done(((f32[8,4,8,128]{3,2,1,0:T(8,128)}), f32[8,4,8,128]{3,2,1,0:T(8,128)S(1)}, u32[]{:S(2)}, u32[]{:S(2)}) %all-to-all-start.5) | async-done | bytes 131104 | tf_op jit(solution)/shard_map/all_to_all | solution.py:379
  139.6 0.0 copy-done.1
  139.6 2.9 %lift.1 = f32[512,128]{1,0:T(8,128)} custom-call(f32[8,4,8,128]{3,2,1,0:T(8,128)S(1)} %all-to-all-done.5.pieces_ref, f32[32,128]{1,0:T(8,128)S(1)} %get-tuple-element.28.held_modes_ref, f32[4096,128]{1,0:T(8,128)S(1)} %bitcast.26, f32[8,128]{1,0:T(8,128)S(1)} %pick.1.small_ref), custom_call_target="tpu_custom_call" | custom-call | tf_op jit(solution)/shard_map/lift/pallas_call | solution.py:433
  142.5 7.9 %all-to-all-start.6 = ((f32[128,4,128]{2,1,0:T(4,128)}), f32[128,4,128]{2,1,0:T(4,128)S(1)}, u32[]{:S(2)}, u32[]{:S(2)}) async-start(f32[128,4,128]{2,1,0:T(4,128)} %bitcast.16), calls=%async_computation.6 | async-start | bytes 524288 | tf_op jit(solution)/shard_map/all_to_all | solution.py:379
  150.4 3.0 %grad.1 = f32[4096,128]{1,0:T(8,128)} custom-call(f32[8,4,8,128]{3,2,1,0:T(8,128)S(1)} %all-to-all-done.5.pieces_ref, f32[32,128]{1,0:T(8,128)S(1)} %get-tuple-element.28.held_modes_ref, f32[8,32]{1,0:T(8,128)S(1)} %pad.7.lift_ref), custom_call_target="tpu_custom_call" | custom-call | tf_op jit(solution)/shard_map/grad/pallas_call | solution.py:434
  153.5 9.8 %all-to-all-done.6 = f32[128,4,128]{2,1,0:T(4,128)S(1)} async-done(((f32[128,4,128]{2,1,0:T(4,128)}), f32[128,4,128]{2,1,0:T(4,128)S(1)}, u32[]{:S(2)}, u32[]{:S(2)}) %all-to-all-start.6) | async-done | bytes 262176 | tf_op jit(solution)/shard_map/all_to_all | solution.py:379
  163.2 0.1 reduce_sum.9.sum_ref
  163.4 0.8 last.1
  (1 shorter events, 0.0 us)
Async XLA Ops:
  0.6 0.9 copy-start.2
  1.6 0.7 copy-start.7
  21.3 13.7 %all-to-all-start.1 = ((f32[8,8,128]{2,1,0:T(8,128)}), f32[8,8,128]{2,1,0:T(8,128)S(1)}, u32[]{:S(2)}, u32[]{:S(2)}) async-start(f32[8,8,128]{2,1,0:T(8,128)} %bitcast.3), calls=%async_computation.1 | async-start | bytes 65536 | tf_op jit(solution)/shard_map/all_to_all | solution.py:379
  35.0 1.6 copy-start
  36.6 21.9 %copy-start.8 = (f32[3,32]{1,0:T(4,128)S(1)}, f32[3,32]{1,0:T(4,128)}, u32[]{:S(2)}) copy-start(f32[3,32]{1,0:T(4,128)} %param.15) | copy-start | bytes 1156
  36.6 21.9 %copy-start.5 = (f32[32,32]{1,0:T(8,128)S(1)}, f32[32,32]{1,0:T(8,128)}, u32[]{:S(2)}) copy-start(f32[32,32]{1,0:T(8,128)} %mix_ref.3) | copy-start | bytes 12292
  36.6 22.0 %copy-start.6 = (s32[8,16]{1,0:T(8,128)S(1)}, s32[8,16]{1,0:T(8,128)}, u32[]{:S(2)}) copy-start(s32[8,16]{1,0:T(8,128)} %mask_ref.1) | copy-start | bytes 1540
  36.6 47.5 %copy-start.3 = (f32[1,3,8,16,128]{4,3,2,1,0:T(8,128)S(1)}, f32[1,3,8,16,128]{4,3,2,1,0:T(8,128)}, u32[]{:S(2)}) copy-start(f32[1,3,8,16,128]{4,3,2,1,0:T(8,128)} %param.8) | copy-start | bytes 589828
  36.6 47.5 %copy-start.4 = (f32[1,3,8,16,128]{4,3,2,1,0:T(8,128)S(1)}, f32[1,3,8,16,128]{4,3,2,1,0:T(8,128)}, u32[]{:S(2)}) copy-start(f32[1,3,8,16,128]{4,3,2,1,0:T(8,128)} %param.9) | copy-start | bytes 589828
  51.3 32.8 %all-to-all-start.3 = ((f32[128,16,128]{2,1,0:T(8,128)}), f32[128,16,128]{2,1,0:T(8,128)S(1)}, u32[]{:S(2)}, u32[]{:S(2)}) async-start(f32[128,16,128]{2,1,0:T(8,128)} %bitcast.10), calls=%async_computation.3 | async-start | bytes 2097152 | tf_op jit(solution)/shard_map/all_to_all | solution.py:379
  92.9 46.7 %copy-start.1 = (f32[2,4,32,2,1024]{4,3,2,1,0:T(2,128)S(1)}, f32[2,4,32,2,1024]{4,3,2,1,0:T(2,128)}, u32[]{:S(2)}) copy-start(f32[2,4,32,2,1024]{4,3,2,1,0:T(2,128)} %param.14) | copy-start | bytes 6291460
  127.0 12.6 %all-to-all-start.5 = ((f32[8,4,8,128]{3,2,1,0:T(8,128)}), f32[8,4,8,128]{3,2,1,0:T(8,128)S(1)}, u32[]{:S(2)}, u32[]{:S(2)}) async-start(f32[8,4,8,128]{3,2,1,0:T(8,128)} %bitcast.15), calls=%async_computation.5 | async-start | bytes 262144 | tf_op jit(solution)/shard_map/all_to_all | solution.py:379
  142.5 20.7 %all-to-all-start.6 = ((f32[128,4,128]{2,1,0:T(4,128)}), f32[128,4,128]{2,1,0:T(4,128)S(1)}, u32[]{:S(2)}, u32[]{:S(2)}) async-start(f32[128,4,128]{2,1,0:T(4,128)} %bitcast.16), calls=%async_computation.6 | async-start | bytes 524288 | tf_op jit(solution)/shard_map/all_to_all | solution.py:379

commit v3 on v2

--- a/solution.py
+++ b/solution.py
@@ -153,7 +153,7 @@
     return jnp.where(iota((32, 1024), 0) == iota((32, 1024), 1) % 32, SCALE, 0.0).astype(BF16)
 
 
-def mix_kernel(freq_ref, pieces_ref, lift_ref, weight_ref, held_modes_ref, out_ref, held_ref):
+def input_planes(freq_ref, pieces_ref, held_modes_ref, held_ref):
     pieces = [pieces_ref[8 * source : 8 * source + 8, :] for source in range(8)]
     rows = split(jnp.concatenate(regroup(pieces), axis=0))
     shape = (N, 128)
@@ -169,6 +169,9 @@
             base = 8 * (4 * parity + channel)
             both.append(held_ref[base : base + 4, :128] + held_ref[base + 4 : base + 8, 128:])
         held_modes_ref[pl.ds(channel, 4, stride=8), :] = jnp.where(first_slot, both[0], both[1])
+
+
+def mix_kernel(held_modes_ref, lift_ref, weight_ref, out_ref):
     lift = lift_spread(lift_ref)
     fold = fold_table()
     for p in range(4):
@@ -183,16 +186,15 @@
             out_ref[target, p] = mixed[start : start + 8]
 
 
-def plane_waves(freq_ref):
+def plane_waves(freq_ref, slot_ref):
     shape = (256, 128)
     row, lane = iota(shape, 0), iota(shape, 1)
     table = wave((row % 128) * freq_ref[1:2, :] + 32 * (lane // 64 - row // 128))
-    parity = lax.axis_index("py") % 2
-    return split(jnp.where(lane // 32 % 2 == parity, table, 0.0))
-
-
-def expand(freq_ref, pieces_ref, out_ref, mark_ref, held_ref):
-    result = dot3(pieces_ref[...], plane_waves(freq_ref), NT)
+    return split(jnp.where(slot_ref[...] == 1, table, 0.0))
+
+
+def expand(freq_ref, slot_ref, pieces_ref, out_hbm, mark_ref, held_ref, out_ref, sems):
+    result = dot3(pieces_ref[...], plane_waves(freq_ref, slot_ref), NT)
     held_ref[:256, :] = result[:, :128]
     held_ref[256:, :] = result[:, 128:]
     parts = []
@@ -202,6 +204,7 @@
         )
     lane = iota((256, 128), 1)
     table = split(wave(rows_waves(freq_ref[0:1, :], lambda part: 32 * (lane // 32 - part)))[:, :64])
+    copies = []
     for pair in range(4):
         wide = jnp.concatenate(
             [
@@ -214,7 +217,14 @@
         for k in range(2):
             start = 256 * (2 * pair + k)
             out_ref[start : start + 256, :] = result[:, 128 * k : 128 * k + 128]
+        rows = pl.ds(512 * pair, 512)
+        copies.append(
+            pltpu.make_async_copy(out_ref.at[rows, :], out_hbm.at[rows, :], sems.at[pair])
+        )
+        copies[pair].start()
     mark_ref[...] = jnp.zeros((8, 128), F32)
+    for copy in copies:
+        copy.wait()
 
 
 def tables_kernel(mark_ref, mask_ref, lift_ref, mix_ref, proj_ref, point_out, proj_out, mask_out):
@@ -277,7 +287,7 @@
         proj_grad[...] += dot2k(error.T[:64], active)
         return carry
 
-    lax.fori_loop(0, 8, plane, 0)
+    lax.fori_loop(0, 8, plane, 0, unroll=8)
 
 
 def pick_kernel(point_grad, proj_grad, small_ref):
@@ -291,7 +301,7 @@
     small_ref[...] = total
 
 
-def reduce_kernel(freq_ref, pieces_ref, out_ref, held_ref):
+def reduce_kernel(freq_ref, slot_ref, pieces_ref, out_ref, held_ref):
     lane = iota((256, 128), 1)
     table = wave(rows_waves(freq_ref[0:1, :], lambda part: 32 * ((lane // 32) % 2 - part)))
     table = split(table.T[:64])
@@ -303,7 +313,7 @@
         for o in range(8):
             held_ref[pl.ds(256 * part + o, 32, stride=8), :] = pieces[o]
     rows = jnp.concatenate([held_ref[:256, :], held_ref[256:, :]], axis=1)
-    out_ref[...] = dot3(rows, plane_waves(freq_ref))
+    out_ref[...] = dot3(rows, plane_waves(freq_ref, slot_ref))
 
 
 def outer_grads(pieces_ref, tile, p):
@@ -314,21 +324,43 @@
 
 
 def lift_kernel(pieces_ref, held_modes_ref, weight_ref, small_ref, sum_ref):
-    tile = fold_table()
+    tile = jnp.where(iota((32, 128), 0) == iota((32, 128), 1) % 32, SCALE, 0.0).astype(BF16)
     tile = jnp.concatenate([tile, tile], axis=0)
-    total = [jnp.zeros((1, 1024), F32)] * 3
+    even = iota((8, 128), 0) % 2 == 0
+    total = [[jnp.zeros((8, 128), F32)] * 2 for channel in range(3)]
     for p in range(4):
         outer = outer_grads(pieces_ref, tile, p)
         real, imag = outer[:64], outer[64:]
-        first, second = weight_rows(weight_ref, 0, p), weight_rows(weight_ref, 1, p)
-        back = jnp.concatenate([first * real + second * imag, first * imag - second * real], axis=0)
         turned = held_modes_ref[8 * p : 8 * p + 8, :].T
+        pairs = []
         for channel in range(3):
-            product = turned[:, channel : channel + 1] * back
-            total[channel] = total[channel] + jnp.sum(product, axis=0, keepdims=True)
-    total = jnp.concatenate(total + [jnp.zeros((5, 1024), F32)], axis=0)
-    place = jnp.where(iota((1024, 128), 0) // 32 + 64 == iota((1024, 128), 1), 1.0, 0.0)
-    total = small_ref[...] + dot3(total, place)
+            first = turned[:64, channel : channel + 1]
+            second = turned[64:, channel : channel + 1]
+            pairs.append((first * real + second * imag, first * imag - second * real))
+        for q in range(32):
+            rows = [
+                [weight_ref[pl.ds(512 * (4 * part + p) + 16 * q + 8 * k, 8), :] for k in range(2)]
+                for part in range(2)
+            ]
+            for channel in range(3):
+                for part in range(2):
+                    pair = pairs[channel][part]
+                    both = jnp.where(even, pair[q : q + 1], pair[32 + q : 33 + q])
+                    for k in range(2):
+                        total[channel][k] = total[channel][k] + both * rows[part][k]
+    lane = iota((128, 128), 1)
+    gather = jnp.where((lane >= 64) & (lane < 96) & (lane % 4 == iota((128, 128), 0) // 32), 1.0, 0.0)
+    owner = (iota((16, 128), 1) - 64) // 4 == iota((16, 128), 0) // 2
+    lines = []
+    for channel in range(3):
+        lines.append(
+            jnp.sum(
+                jnp.where(owner, dot3(jnp.concatenate(total[channel], axis=0), gather), 0.0),
+                axis=0,
+                keepdims=True,
+            )
+        )
+    total = small_ref[...] + jnp.concatenate(lines + [jnp.zeros((5, 128), F32)], axis=0)
     total = jnp.where(iota((8, 128), 0) < 4, total, pltpu.roll(total, 4, 0))
     for target in range(64):
         sum_ref[8 * target : 8 * target + 8, :] = total
@@ -361,13 +393,17 @@
     proj_out[...] = total[:3, 32:64]
 
 
-def call(kernel, shapes, scratch=(), name=None):
+def call(kernel, shapes, scratch=(), places=None, name=None):
+    specs = {}
+    if places is not None:
+        specs["out_specs"] = tuple(pl.BlockSpec(memory_space=place) for place in places)
     return pl.pallas_call(
         kernel,
         out_shape=shapes,
         scratch_shapes=list(scratch),
         name=name,
         compiler_params=pltpu.CompilerParams(vmem_limit_bytes=48 * 1024 * 1024),
+        **specs,
     )
 
 
@@ -389,6 +425,8 @@
     spectral_weight,
     proj_weight,
 ):
+    slot = jnp.arange(128, dtype=jnp.int32) // 32 % 2 == lax.axis_index("py") % 2
+    slot = slot.astype(jnp.int32)[None]
     field = input_field[0]
     target = target_field[0]
     weight = spectral_weight.reshape(2, 4, 32, 2, 8, 128).transpose(0, 1, 2, 4, 3, 5)
@@ -404,19 +442,22 @@
     pieces = exchange(pieces.reshape(16, 16, 128), "px").reshape(256, 128)
     pieces = call(input_rows, array(64, 128), name="input_rows")(freq, pieces)
     pieces = exchange(pieces.reshape(8, 8, 128), "py").reshape(64, 128)
-    held_modes, pieces = call(
-        mix_kernel,
-        (array(32, 128), array(8, 4, 8, 128)),
-        [pltpu.VMEM((64, 256), F32)],
-        name="mix",
-    )(freq, pieces, lift_rows, weight)
+    held_modes = call(
+        input_planes, array(32, 128), [pltpu.VMEM((64, 256), F32)], name="input_planes"
+    )(freq, pieces)
+    pieces = call(mix_kernel, array(8, 4, 8, 128), name="mix")(held_modes, lift_rows, weight)
     pieces = exchange(pieces, "py").reshape(256, 128)
     pieces, mark = call(
         expand,
         (array(2048, 128), array(8, 128)),
-        [pltpu.VMEM((512, 128), F32)],
+        [
+            pltpu.VMEM((512, 128), F32),
+            pltpu.VMEM((2048, 128), F32),
+            pltpu.SemaphoreType.DMA((4,)),
+        ],
+        (pltpu.HBM, pltpu.VMEM),
         name="expand",
-    )(freq, pieces)
+    )(freq, slot, pieces)
     point, proj, mask = call(
         tables_kernel, (array(64, 512), array(128, 512), array(8, 128)), name="tables"
     )(mark, row_mask, lift_rows, mix_weight, proj_rows)
@@ -427,7 +468,7 @@
     small = call(pick_kernel, array(8, 128), name="pick")(point_grad, proj_grad)
     pieces = exchange(pieces.reshape(128, 16, 128), ("py", "px")).reshape(2048, 128)
     pieces = call(reduce_kernel, array(256, 128), [pltpu.VMEM((512, 128), F32)], name="reduce")(
-        freq, pieces
+        freq, slot, pieces
     )
     pieces = exchange(pieces.reshape(8, 4, 8, 128), "py")
     sums = call(lift_kernel, array(512, 128), name="lift")(pieces, held_modes, weight, small)

time: 165 us -> 164 us (level)
  blocking collectives: 60 us -> 49.7 us
  waiting for transfers between devices: 49.1 us -> 56.9 us
  starting transfers between devices: 25.8 us -> 29.1 us
  Pallas kernels: 24.5 us -> 22.8 us
    all_to_all x3 -> x2, blocking collectives: 60 us -> 49.7 us  [exchange(): return lax.all_to_all(value, axes, split_axis=0, concat_axis=0, tiled=True)]
    all_to_all x4 -> x5, waiting for transfers between devices: 49.1 us -> 56.9 us  [exchange(): return lax.all_to_all(value, axes, split_axis=0, concat_axis=0, tiled=True)]
    all_to_all x4 -> x5, starting transfers between devices: 25.8 us -> 29.1 us  [exchange(): return lax.all_to_all(value, axes, split_axis=0, concat_axis=0, tiled=True)]
    pallas_call x1, Pallas kernels: 8.73 us -> 6.9 us  [body(): call(grid_kernel, (array(2048, 128), array(64, 512), array(64, 512)), nam...]
  transfers between devices with their start and end apart: 4 -> 5, of which waited for: 4 -> 5; matrix products, arithmetic and copies ran while one was open for 0% -> 0% of each run, Pallas kernels for 3% -> 3%
where the time goes in v3:
time: 164 us; the launch traced here: 163 us
  waiting for transfers between devices  56.9 us (35%)
  blocking collectives  49.7 us (30%)
  starting transfers between devices  29.1 us (18%)
  Pallas kernels  22.8 us (14%)
  local copies, waits for them, and re-layouts  3.91 us (2%)
    all_to_all x5, waiting for transfers between devices, exchange(): return lax.all_to_all(value, axes, split_axis=0, concat_axis=0, tiled=True)  56.9 us
    all_to_all x2, blocking collectives, exchange(): return lax.all_to_all(value, axes, split_axis=0, concat_axis=0, tiled=True)  49.7 us
    all_to_all x5, starting transfers between devices, exchange(): return lax.all_to_all(value, axes, split_axis=0, concat_axis=0, tiled=True)  29.1 us
    pallas_call x1, Pallas kernels, body(): call(grid_kernel, (array(2048, 128), array(64, 512), array(64, 512)), nam...  6.9 us
  transfers between devices with their start and end apart: 5, of which 5 were waited for; matrix products, arithmetic and copies ran while one was open for 0% of the time, Pallas kernels for 3%

profile of v3, /device:TPU:8, one launch (start us, length us, event | category | flops | bytes accessed | tf_op | source)
XLA Modules:
  0.0 163.4 jit_solution(10677932491027254355)
XLA Ops:
  0.6 0.0 copy-start.2
  0.6 0.9 copy-done.2
  1.6 0.0 copy-start.7
  1.6 0.7 copy-done.7
  2.2 0.8 input_depth.1
  3.0 17.3 %all_to_all.35 = f32[16,16,128]{2,1,0:T(8,128)S(1)} all-to-all(f32[16,16,128]{2,1,0:T(8,128)S(1)} %bitcast.35), channel_id=1, replica_groups=mesh['seed'=2,'px'=16,'py'=8] {'px'}, dimensions={0} | all-to-all | bytes 262144 | tf_op jit(solution)/shard_map/all_to_all | solution.py:415
  20.3 1.0 input_rows.1
  21.3 6.0 %all-to-all-start.1 = ((f32[8,8,128]{2,1,0:T(8,128)}), f32[8,8,128]{2,1,0:T(8,128)S(1)}, u32[]{:S(2)}, u32[]{:S(2)}) async-start(f32[8,8,128]{2,1,0:T(8,128)} %bitcast.3), calls=%async_computation.1 | async-start | bytes 65536 | tf_op jit(solution)/shard_map/all_to_all | solution.py:415
  27.3 0.7 pad.7.lift_ref
  28.0 7.0 %all-to-all-done.1 = f32[8,8,128]{2,1,0:T(8,128)S(1)} async-done(((f32[8,8,128]{2,1,0:T(8,128)}), f32[8,8,128]{2,1,0:T(8,128)S(1)}, u32[]{:S(2)}, u32[]{:S(2)}) %all-to-all-start.1) | async-done | bytes 32800 | tf_op jit(solution)/shard_map/all_to_all | solution.py:415
  35.0 0.3 input_planes.1.held_modes_ref
  35.3 0.0 copy-start
  35.3 1.6 copy-done
  36.9 0.0 copy-start.8
  36.9 0.0 copy-start.5
  36.9 0.0 copy-start.6
  36.9 0.0 copy-start.3
  36.9 0.0 copy-start.4
  36.9 2.7 %mix.1 = f32[8,4,8,128]{3,2,1,0:T(8,128)} custom-call(f32[32,128]{1,0:T(8,128)S(1)} %input_planes.1.held_modes_ref, f32[8,32]{1,0:T(8,128)S(1)} %pad.7.lift_ref, f32[4096,128]{1,0:T(8,128)S(1)} %bitcast.25), custom_call_target="tpu_custom_call" | custom-call | tf_op jit(solution)/shard_map/mix/pallas_call | solution.py:448
  39.7 3.4 %all-to-all-start.2 = ((f32[8,4,8,128]{3,2,1,0:T(8,128)}), f32[8,4,8,128]{3,2,1,0:T(8,128)S(1)}, u32[]{:S(2)}, u32[]{:S(2)}) async-start(f32[8,4,8,128]{3,2,1,0:T(8,128)} %mix.1), calls=%async_computation.2 | async-start | bytes 262144 | tf_op jit(solution)/shard_map/all_to_all | solution.py:415
  43.1 7.8 %all-to-all-done.2 = f32[8,4,8,128]{3,2,1,0:T(8,128)S(1)} async-done(((f32[8,4,8,128]{3,2,1,0:T(8,128)}), f32[8,4,8,128]{3,2,1,0:T(8,128)S(1)}, u32[]{:S(2)}, u32[]{:S(2)}) %all-to-all-start.2) | async-done | bytes 131104 | tf_op jit(solution)/shard_map/all_to_all | solution.py:415
  50.9 2.2 %expand.1 = (f32[2048,128]{1,0:T(8,128)}, f32[8,128]{1,0:T(8,128)S(1)}) custom-call(s32[8,128]{1,0:T(8,128)S(1)} %get-tuple-element.17.freq_ref, s32[1,128]{1,0:T(1,128)S(1)} %compare_convert_fusion.slot_ref, f32[256,128]{1,0:T(8,128)S(1)} %bitcast.32), custom_call_target="tpu_custom_call" | custom-call | tf_op jit(solution)/shard_map/expand/pallas_call | solution.py:450
  53.1 7.2 %all-to-all-start.3 = ((f32[128,16,128]{2,1,0:T(8,128)}), f32[128,16,128]{2,1,0:T(8,128)S(1)}, u32[]{:S(2)}, u32[]{:S(2)}) async-start(f32[128,16,128]{2,1,0:T(8,128)} %bitcast.10), calls=%async_computation.3 | async-start | bytes 2097152 | tf_op jit(solution)/shard_map/all_to_all | solution.py:415
  60.3 0.0 copy-done.8
  60.3 0.0 copy-done.5
  60.3 0.0 copy-done.6
  60.3 0.6 tables.1
  60.9 24.9 %all-to-all-done.3 = f32[128,16,128]{2,1,0:T(8,128)S(1)} async-done(((f32[128,16,128]{2,1,0:T(8,128)}), f32[128,16,128]{2,1,0:T(8,128)S(1)}, u32[]{:S(2)}, u32[]{:S(2)}) %all-to-all-start.3) | async-done | bytes 1048608 | tf_op jit(solution)/shard_map/all_to_all | solution.py:415
  85.8 0.0 copy-done.3
  85.8 0.0 copy-done.4
  85.8 6.9 %grid.1 = (f32[2048,128]{1,0:T(8,128)S(1)}, f32[64,512]{1,0:T(8,128)S(1)}, f32[64,512]{1,0:T(8,128)S(1)}) custom-call(s32[8,128]{1,0:T(8,128)S(1)} %get-tuple-element.17.freq_ref, f32[2048,128]{1,0:T(8,128)S(1)} %bitcast.27, f32[3,8,16,128]{3,2,1,0:T(8,128)S(1)} %bitcast.31, f32[3,8,16,128]{3,2,1,0:T(8,128)S(1)} %bitcast.34, ...), custom_call_target="tpu_custom_call" | custom-call | tf_op jit(solution)/shard_map/grid/pallas_call | solution.py:465
  92.7 0.0 copy-start.1
  92.8 32.4 %all_to_all.36 = f32[128,16,128]{2,1,0:T(8,128)S(1)} all-to-all(f32[128,16,128]{2,1,0:T(8,128)S(1)} %bitcast.29), channel_id=1, replica_groups=mesh['seed'=2,'px'=16,'py'=8] {'py','px'}, dimensions={0} | all-to-all | bytes 2097152 | tf_op jit(solution)/shard_map/all_to_all | solution.py:415
  125.1 1.8 %reduce.1 = f32[256,128]{1,0:T(8,128)} custom-call(s32[8,128]{1,0:T(8,128)S(1)} %get-tuple-element.17.freq_ref, s32[1,128]{1,0:T(1,128)S(1)} %compare_convert_fusion.slot_ref, f32[2048,128]{1,0:T(8,128)S(1)} %bitcast.28), custom_call_target="tpu_custom_call" | custom-call | tf_op jit(solution)/shard_map/reduce/pallas_call | solution.py:470
  126.9 4.7 %all-to-all-start.5 = ((f32[8,4,8,128]{3,2,1,0:T(8,128)}), f32[8,4,8,128]{3,2,1,0:T(8,128)S(1)}, u32[]{:S(2)}, u32[]{:S(2)}) async-start(f32[8,4,8,128]{3,2,1,0:T(8,128)} %bitcast.15), calls=%async_computation.5 | async-start | bytes 262144 | tf_op jit(solution)/shard_map/all_to_all | solution.py:415
  131.6 0.5 pick.1.small_ref
  132.1 7.4 %all-to-all-done.5.pieces_ref = f32[8,4,8,128]{3,2,1,0:T(8,128)S(1)} async-done(((f32[8,4,8,128]{3,2,1,0:T(8,128)}), f32[8,4,8,128]{3,2,1,0:T(8,128)S(1)}, u32[]{:S(2)}, u32[]{:S(2)}) %all-to-all-start.5) | async-done | bytes 131104 | tf_op jit(solution)/shard_map/all_to_all | solution.py:415
  139.5 0.0 copy-done.1
  139.5 2.2 %lift.1 = f32[512,128]{1,0:T(8,128)} custom-call(f32[8,4,8,128]{3,2,1,0:T(8,128)S(1)} %all-to-all-done.5.pieces_ref, f32[32,128]{1,0:T(8,128)S(1)} %input_planes.1.held_modes_ref, f32[4096,128]{1,0:T(8,128)S(1)} %bitcast.26, f32[8,128]{1,0:T(8,128)S(1)} %pick.1.small_ref), custom_call_target="tpu_custom_call" | custom-call | tf_op jit(solution)/shard_map/lift/pallas_call | solution.py:474
  141.7 7.9 %all-to-all-start.6 = ((f32[128,4,128]{2,1,0:T(4,128)}), f32[128,4,128]{2,1,0:T(4,128)S(1)}, u32[]{:S(2)}, u32[]{:S(2)}) async-start(f32[128,4,128]{2,1,0:T(4,128)} %bitcast.16), calls=%async_computation.6 | async-start | bytes 524288 | tf_op jit(solution)/shard_map/all_to_all | solution.py:415
  149.6 3.0 %grad.1 = f32[4096,128]{1,0:T(8,128)} custom-call(f32[8,4,8,128]{3,2,1,0:T(8,128)S(1)} %all-to-all-done.5.pieces_ref, f32[32,128]{1,0:T(8,128)S(1)} %input_planes.1.held_modes_ref, f32[8,32]{1,0:T(8,128)S(1)} %pad.7.lift_ref), custom_call_target="tpu_custom_call" | custom-call | tf_op jit(solution)/shard_map/grad/pallas_call | solution.py:475
  152.7 9.8 %all-to-all-done.6 = f32[128,4,128]{2,1,0:T(4,128)S(1)} async-done(((f32[128,4,128]{2,1,0:T(4,128)}), f32[128,4,128]{2,1,0:T(4,128)S(1)}, u32[]{:S(2)}, u32[]{:S(2)}) %all-to-all-start.6) | async-done | bytes 262176 | tf_op jit(solution)/shard_map/all_to_all | solution.py:415
  162.4 0.1 reduce_sum.9.sum_ref
  162.6 0.8 last.1
  (2 shorter events, 0.0 us)
Async XLA Ops:
  0.6 0.9 copy-start.2
  1.6 0.7 copy-start.7
  21.3 13.7 %all-to-all-start.1 = ((f32[8,8,128]{2,1,0:T(8,128)}), f32[8,8,128]{2,1,0:T(8,128)S(1)}, u32[]{:S(2)}, u32[]{:S(2)}) async-start(f32[8,8,128]{2,1,0:T(8,128)} %bitcast.3), calls=%async_computation.1 | async-start | bytes 65536 | tf_op jit(solution)/shard_map/all_to_all | solution.py:415
  35.3 1.6 copy-start
  36.9 23.3 %copy-start.8 = (f32[3,32]{1,0:T(4,128)S(1)}, f32[3,32]{1,0:T(4,128)}, u32[]{:S(2)}) copy-start(f32[3,32]{1,0:T(4,128)} %param.15) | copy-start | bytes 1156
  36.9 23.4 %copy-start.5 = (f32[32,32]{1,0:T(8,128)S(1)}, f32[32,32]{1,0:T(8,128)}, u32[]{:S(2)}) copy-start(f32[32,32]{1,0:T(8,128)} %mix_ref.3) | copy-start | bytes 12292
  36.9 23.4 %copy-start.6 = (s32[8,16]{1,0:T(8,128)S(1)}, s32[8,16]{1,0:T(8,128)}, u32[]{:S(2)}) copy-start(s32[8,16]{1,0:T(8,128)} %mask_ref.1) | copy-start | bytes 1540
  36.9 48.9 %copy-start.3 = (f32[1,3,8,16,128]{4,3,2,1,0:T(8,128)S(1)}, f32[1,3,8,16,128]{4,3,2,1,0:T(8,128)}, u32[]{:S(2)}) copy-start(f32[1,3,8,16,128]{4,3,2,1,0:T(8,128)} %param.8) | copy-start | bytes 589828
  36.9 48.9 %copy-start.4 = (f32[1,3,8,16,128]{4,3,2,1,0:T(8,128)S(1)}, f32[1,3,8,16,128]{4,3,2,1,0:T(8,128)}, u32[]{:S(2)}) copy-start(f32[1,3,8,16,128]{4,3,2,1,0:T(8,128)} %param.9) | copy-start | bytes 589828
  39.7 11.2 %all-to-all-start.2 = ((f32[8,4,8,128]{3,2,1,0:T(8,128)}), f32[8,4,8,128]{3,2,1,0:T(8,128)S(1)}, u32[]{:S(2)}, u32[]{:S(2)}) async-start(f32[8,4,8,128]{3,2,1,0:T(8,128)} %mix.1), calls=%async_computation.2 | async-start | bytes 262144 | tf_op jit(solution)/shard_map/all_to_all | solution.py:415
  53.1 32.8 %all-to-all-start.3 = ((f32[128,16,128]{2,1,0:T(8,128)}), f32[128,16,128]{2,1,0:T(8,128)S(1)}, u32[]{:S(2)}, u32[]{:S(2)}) async-start(f32[128,16,128]{2,1,0:T(8,128)} %bitcast.10), calls=%async_computation.3 | async-start | bytes 2097152 | tf_op jit(solution)/shard_map/all_to_all | solution.py:415
  92.7 46.7 %copy-start.1 = (f32[2,4,32,2,1024]{4,3,2,1,0:T(2,128)S(1)}, f32[2,4,32,2,1024]{4,3,2,1,0:T(2,128)}, u32[]{:S(2)}) copy-start(f32[2,4,32,2,1024]{4,3,2,1,0:T(2,128)} %param.14) | copy-start | bytes 6291460
  126.9 12.6 %all-to-all-start.5 = ((f32[8,4,8,128]{3,2,1,0:T(8,128)}), f32[8,4,8,128]{3,2,1,0:T(8,128)S(1)}, u32[]{:S(2)}, u32[]{:S(2)}) async-start(f32[8,4,8,128]{3,2,1,0:T(8,128)} %bitcast.15), calls=%async_computation.5 | async-start | bytes 262144 | tf_op jit(solution)/shard_map/all_to_all | solution.py:415
  141.7 20.7 %all-to-all-start.6 = ((f32[128,4,128]{2,1,0:T(4,128)}), f32[128,4,128]{2,1,0:T(4,128)S(1)}, u32[]{:S(2)}, u32[]{:S(2)}) async-start(f32[128,4,128]{2,1,0:T(4,128)} %bitcast.16), calls=%async_computation.6 | async-start | bytes 524288 | tf_op jit(solution)/shard_map/all_to_all | solution.py:415

commit v4 on v3

--- a/solution.py
+++ b/solution.py
@@ -153,7 +153,7 @@
     return jnp.where(iota((32, 1024), 0) == iota((32, 1024), 1) % 32, SCALE, 0.0).astype(BF16)
 
 
-def input_planes(freq_ref, pieces_ref, held_modes_ref, held_ref):
+def mix_kernel(freq_ref, pieces_ref, lift_ref, weight_ref, held_modes_ref, out_ref, held_ref):
     pieces = [pieces_ref[8 * source : 8 * source + 8, :] for source in range(8)]
     rows = split(jnp.concatenate(regroup(pieces), axis=0))
     shape = (N, 128)
@@ -169,9 +169,6 @@
             base = 8 * (4 * parity + channel)
             both.append(held_ref[base : base + 4, :128] + held_ref[base + 4 : base + 8, 128:])
         held_modes_ref[pl.ds(channel, 4, stride=8), :] = jnp.where(first_slot, both[0], both[1])
-
-
-def mix_kernel(held_modes_ref, lift_ref, weight_ref, out_ref):
     lift = lift_spread(lift_ref)
     fold = fold_table()
     for p in range(4):
@@ -186,15 +183,16 @@
             out_ref[target, p] = mixed[start : start + 8]
 
 
-def plane_waves(freq_ref, slot_ref):
+def plane_waves(freq_ref):
     shape = (256, 128)
     row, lane = iota(shape, 0), iota(shape, 1)
     table = wave((row % 128) * freq_ref[1:2, :] + 32 * (lane // 64 - row // 128))
-    return split(jnp.where(slot_ref[...] == 1, table, 0.0))
-
-
-def expand(freq_ref, slot_ref, pieces_ref, out_hbm, mark_ref, held_ref, out_ref, sems):
-    result = dot3(pieces_ref[...], plane_waves(freq_ref, slot_ref), NT)
+    parity = lax.axis_index("py") % 2
+    return split(jnp.where(lane // 32 % 2 == parity, table, 0.0))
+
+
+def expand(freq_ref, pieces_ref, out_hbm, mark_ref, held_ref, out_ref, sems):
+    result = dot3(pieces_ref[...], plane_waves(freq_ref), NT)
     held_ref[:256, :] = result[:, :128]
     held_ref[256:, :] = result[:, 128:]
     parts = []
@@ -230,12 +228,15 @@
 def tables_kernel(mark_ref, mask_ref, lift_ref, mix_ref, proj_ref, point_out, proj_out, mask_out):
     pick = jnp.where(iota((32, 512), 0) == iota((32, 512), 1) // 16, 1.0, 0.0).astype(BF16)
     same = iota((64, 512), 0) % 16 == iota((64, 512), 1) % 16
-    rows = jnp.where(iota((64, 8), 0) // 16 == iota((64, 8), 1), 1.0, 0.0).astype(BF16)
+    owner = iota((64, 512), 0) // 16
 
     def spread(matrix):
         high, low = split(matrix)
-        wide = split(mul(high, pick, NN) + mul(low, pick, NN))
-        return jnp.where(same, mul(rows, wide[0], NN) + mul(rows, wide[1], NN), 0.0)
+        wide = mul(high, pick, NN) + mul(low, pick, NN)
+        total = jnp.zeros((64, 512), F32)
+        for channel in range(3):
+            total = jnp.where(same & (owner == channel), wide[channel : channel + 1], total)
+        return total
 
     point_out[...] = spread(dot3(lift_ref[...], mix_ref[...], NT))
     table = spread(proj_ref[...])
@@ -301,7 +302,7 @@
     small_ref[...] = total
 
 
-def reduce_kernel(freq_ref, slot_ref, pieces_ref, out_ref, held_ref):
+def reduce_kernel(freq_ref, pieces_ref, out_ref, held_ref):
     lane = iota((256, 128), 1)
     table = wave(rows_waves(freq_ref[0:1, :], lambda part: 32 * ((lane // 32) % 2 - part)))
     table = split(table.T[:64])
@@ -313,7 +314,7 @@
         for o in range(8):
             held_ref[pl.ds(256 * part + o, 32, stride=8), :] = pieces[o]
     rows = jnp.concatenate([held_ref[:256, :], held_ref[256:, :]], axis=1)
-    out_ref[...] = dot3(rows, plane_waves(freq_ref, slot_ref))
+    out_ref[...] = dot3(rows, plane_waves(freq_ref))
 
 
 def outer_grads(pieces_ref, tile, p):
@@ -388,7 +389,11 @@
 def last_kernel(sum_ref, lift_ref, mix_ref, lift_out, mix_out, proj_out):
     total = jnp.concatenate([sum_ref[...], jnp.zeros((124, 128), F32)], axis=0) * SCALE
     cross = total[:8, :32]
-    mix_out[...] = dot3(total.T[:32, :8], lift_ref[...])
+    turned = total.T[:32]
+    mixed = turned[:, 0:1] * lift_ref[0:1]
+    for channel in (1, 2):
+        mixed = mixed + turned[:, channel : channel + 1] * lift_ref[channel : channel + 1]
+    mix_out[...] = mixed
     lift_out[...] = (dot3(cross, mix_ref[...]) + total[:8, 64:96])[:3]
     proj_out[...] = total[:3, 32:64]
 
@@ -425,14 +430,11 @@
     spectral_weight,
     proj_weight,
 ):
-    slot = jnp.arange(128, dtype=jnp.int32) // 32 % 2 == lax.axis_index("py") % 2
-    slot = slot.astype(jnp.int32)[None]
     field = input_field[0]
     target = target_field[0]
     weight = spectral_weight.reshape(2, 4, 32, 2, 8, 128).transpose(0, 1, 2, 4, 3, 5)
     weight = weight.reshape(4096, 128)
-    lift_rows = jnp.pad(lift_weight.T, ((0, 5), (0, 0)))
-    proj_rows = jnp.pad(proj_weight, ((0, 5), (0, 0)))
+    lift_rows = lift_weight.T
 
     freq, pieces = call(
         input_depth,
@@ -442,10 +444,12 @@
     pieces = exchange(pieces.reshape(16, 16, 128), "px").reshape(256, 128)
     pieces = call(input_rows, array(64, 128), name="input_rows")(freq, pieces)
     pieces = exchange(pieces.reshape(8, 8, 128), "py").reshape(64, 128)
-    held_modes = call(
-        input_planes, array(32, 128), [pltpu.VMEM((64, 256), F32)], name="input_planes"
-    )(freq, pieces)
-    pieces = call(mix_kernel, array(8, 4, 8, 128), name="mix")(held_modes, lift_rows, weight)
+    held_modes, pieces = call(
+        mix_kernel,
+        (array(32, 128), array(8, 4, 8, 128)),
+        [pltpu.VMEM((64, 256), F32)],
+        name="mix",
+    )(freq, pieces, lift_rows, weight)
     pieces = exchange(pieces, "py").reshape(256, 128)
     pieces, mark = call(
         expand,
@@ -457,10 +461,10 @@
         ],
         (pltpu.HBM, pltpu.VMEM),
         name="expand",
-    )(freq, slot, pieces)
+    )(freq, pieces)
     point, proj, mask = call(
         tables_kernel, (array(64, 512), array(128, 512), array(8, 128)), name="tables"
-    )(mark, row_mask, lift_rows, mix_weight, proj_rows)
+    )(mark, row_mask, lift_rows, mix_weight, proj_weight)
     pieces = exchange(pieces.reshape(128, 16, 128), ("py", "px")).reshape(2048, 128)
     pieces, point_grad, proj_grad = call(
         grid_kernel, (array(2048, 128), array(64, 512), array(64, 512)), name="grid"
@@ -468,7 +472,7 @@
     small = call(pick_kernel, array(8, 128), name="pick")(point_grad, proj_grad)
     pieces = exchange(pieces.reshape(128, 16, 128), ("py", "px")).reshape(2048, 128)
     pieces = call(reduce_kernel, array(256, 128), [pltpu.VMEM((512, 128), F32)], name="reduce")(
-        freq, slot, pieces
+        freq, pieces
     )
     pieces = exchange(pieces.reshape(8, 4, 8, 128), "py")
     sums = call(lift_kernel, array(512, 128), name="lift")(pieces, held_modes, weight, small)

time: 164 us -> 162 us (0.988)
  blocking collectives: 49.7 us -> 73.5 us
  waiting for transfers between devices: 56.9 us -> 42.4 us
  starting transfers between devices: 29.1 us -> 19.8 us
  Pallas kernels: 22.8 us -> 20.9 us
    all_to_all x2 -> x4, blocking collectives: 49.7 us -> 73.5 us  [exchange(): return lax.all_to_all(value, axes, split_axis=0, concat_axis=0, tiled=True)]
    all_to_all x5 -> x3, waiting for transfers between devices: 56.9 us -> 42.4 us  [exchange(): return lax.all_to_all(value, axes, split_axis=0, concat_axis=0, tiled=True)]
    all_to_all x5 -> x3, starting transfers between devices: 29.1 us -> 19.8 us  [exchange(): return lax.all_to_all(value, axes, split_axis=0, concat_axis=0, tiled=True)]
    unnamed x18 -> x22, local copies, waits for them, and re-layouts: 3.22 us -> 3.91 us
  transfers between devices with their start and end apart: 5 -> 3, of which waited for: 5 -> 3; matrix products, arithmetic and copies ran while one was open for 0% -> 0% of each run, Pallas kernels for 3% -> 2%
where the time goes in v4:
time: 162 us; the launch traced here: 161 us
  blocking collectives  73.5 us (45%)
  waiting for transfers between devices  42.4 us (26%)
  Pallas kernels  20.9 us (13%)
  starting transfers between devices  19.8 us (12%)
  local copies, waits for them, and re-layouts  3.91 us (2%)
    all_to_all x4, blocking collectives, exchange(): return lax.all_to_all(value, axes, split_axis=0, concat_axis=0, tiled=True)  73.5 us
    all_to_all x3, waiting for transfers between devices, exchange(): return lax.all_to_all(value, axes, split_axis=0, concat_axis=0, tiled=True)  42.4 us
    all_to_all x3, starting transfers between devices, exchange(): return lax.all_to_all(value, axes, split_axis=0, concat_axis=0, tiled=True)  19.8 us
    pallas_call x1, Pallas kernels, body(): call(grid_kernel, (array(2048, 128), array(64, 512), array(64, 512)), nam...  6.9 us
    unnamed x22, local copies, waits for them, and re-layouts  3.91 us
  transfers between devices with their start and end apart: 3, of which 3 were waited for; matrix products, arithmetic and copies ran while one was open for 0% of the time, Pallas kernels for 2%

profile of v4, /device:TPU:8, one launch (start us, length us, event | category | flops | bytes accessed | tf_op | source)
XLA Modules:
  0.0 161.4 jit_solution(9608662198081617539)
XLA Ops:
  0.6 0.0 copy-start.2
  0.6 0.9 copy-done.2
  1.6 0.0 copy-start.9
  1.6 0.7 copy-done.9
  2.2 0.8 input_depth.1
  3.0 17.3 %all_to_all.35 = f32[16,16,128]{2,1,0:T(8,128)S(1)} all-to-all(f32[16,16,128]{2,1,0:T(8,128)S(1)} %bitcast.36), channel_id=1, replica_groups=mesh['seed'=2,'px'=16,'py'=8] {'px'}, dimensions={0} | all-to-all | bytes 262144 | tf_op jit(solution)/shard_map/all_to_all | solution.py:420
  20.3 0.3 input_rows.1
  20.7 13.5 %all_to_all.36 = f32[8,8,128]{2,1,0:T(8,128)S(1)} all-to-all(f32[8,8,128]{2,1,0:T(8,128)S(1)} %bitcast.37), channel_id=1, replica_groups=mesh['seed'=2,'px'=16,'py'=8] {'py'}, dimensions={0} | all-to-all | bytes 65536 | tf_op jit(solution)/shard_map/all_to_all | solution.py:420
  34.2 0.0 copy-start
  34.2 1.6 copy-done
  35.8 0.0 copy-start.6
  35.8 0.7 copy-done.6
  36.5 0.0 copy-start.5
  36.5 0.0 copy-start.7
  36.5 0.0 copy-start.8
  36.5 0.0 copy-start.10
  36.5 0.0 copy-start.3
  36.5 0.0 copy-start.4
  36.5 2.1 %mix.1 = (f32[32,128]{1,0:T(8,128)S(1)}, f32[8,4,8,128]{3,2,1,0:T(8,128)S(1)}) custom-call(s32[8,128]{1,0:T(8,128)S(1)} %get-tuple-element.19.freq_ref, f32[64,128]{1,0:T(8,128)S(1)} %bitcast.35, f32[3,32]{1,0:T(4,128)S(1)} %bitcast.38, f32[4096,128]{1,0:T(8,128)S(1)} %bitcast.25), custom_call_target="tpu_custom_call" | custom-call | tf_op jit(solution)/shard_map/mix/pallas_call | solution.py:447
  38.6 10.3 %all_to_all.37 = f32[8,4,8,128]{3,2,1,0:T(8,128)S(1)} all-to-all(f32[8,4,8,128]{3,2,1,0:T(8,128)S(1)} %get-tuple-element.21), channel_id=1, replica_groups=mesh['seed'=2,'px'=16,'py'=8] {'py'}, dimensions={0} | all-to-all | bytes 262144 | tf_op jit(solution)/shard_map/all_to_all | solution.py:420
  48.9 2.2 %expand.1 = (f32[2048,128]{1,0:T(8,128)}, f32[8,128]{1,0:T(8,128)S(1)}) custom-call(s32[8,128]{1,0:T(8,128)S(1)} %get-tuple-element.19.freq_ref, f32[256,128]{1,0:T(8,128)S(1)} %bitcast.32), custom_call_target="tpu_custom_call" | custom-call | tf_op jit(solution)/shard_map/expand/pallas_call | solution.py:454
  51.1 7.2 %all-to-all-start.3 = ((f32[128,16,128]{2,1,0:T(8,128)}), f32[128,16,128]{2,1,0:T(8,128)S(1)}, u32[]{:S(2)}, u32[]{:S(2)}) async-start(f32[128,16,128]{2,1,0:T(8,128)} %bitcast.10), calls=%async_computation.3 | async-start | bytes 2097152 | tf_op jit(solution)/shard_map/all_to_all | solution.py:420
  58.3 0.0 copy-done.5
  58.3 0.0 copy-done.7
  58.3 0.0 copy-done.8
  58.3 0.0 copy-done.10
  58.3 0.3 tables.1
  58.6 25.2 %all-to-all-done.3 = f32[128,16,128]{2,1,0:T(8,128)S(1)} async-done(((f32[128,16,128]{2,1,0:T(8,128)}), f32[128,16,128]{2,1,0:T(8,128)S(1)}, u32[]{:S(2)}, u32[]{:S(2)}) %all-to-all-start.3) | async-done | bytes 1048608 | tf_op jit(solution)/shard_map/all_to_all | solution.py:420
  83.8 0.0 copy-done.3
  83.8 0.0 copy-done.4
  83.8 6.9 %grid.1 = (f32[2048,128]{1,0:T(8,128)S(1)}, f32[64,512]{1,0:T(8,128)S(1)}, f32[64,512]{1,0:T(8,128)S(1)}) custom-call(s32[8,128]{1,0:T(8,128)S(1)} %get-tuple-element.19.freq_ref, f32[2048,128]{1,0:T(8,128)S(1)} %bitcast.27, f32[3,8,16,128]{3,2,1,0:T(8,128)S(1)} %bitcast.31, f32[3,8,16,128]{3,2,1,0:T(8,128)S(1)} %bitcast.34, ...), custom_call_target="tpu_custom_call" | custom-call | tf_op jit(solution)/shard_map/grid/pallas_call | solution.py:469
  90.7 0.0 copy-start.1
  90.8 32.4 %all_to_all.38 = f32[128,16,128]{2,1,0:T(8,128)S(1)} all-to-all(f32[128,16,128]{2,1,0:T(8,128)S(1)} %bitcast.29), channel_id=1, replica_groups=mesh['seed'=2,'px'=16,'py'=8] {'py','px'}, dimensions={0} | all-to-all | bytes 2097152 | tf_op jit(solution)/shard_map/all_to_all | solution.py:420
  123.1 1.8 %reduce.1 = f32[256,128]{1,0:T(8,128)} custom-call(s32[8,128]{1,0:T(8,128)S(1)} %get-tuple-element.19.freq_ref, f32[2048,128]{1,0:T(8,128)S(1)} %bitcast.28), custom_call_target="tpu_custom_call" | custom-call | tf_op jit(solution)/shard_map/reduce/pallas_call | solution.py:474
  124.9 4.7 %all-to-all-start.5 = ((f32[8,4,8,128]{3,2,1,0:T(8,128)}), f32[8,4,8,128]{3,2,1,0:T(8,128)S(1)}, u32[]{:S(2)}, u32[]{:S(2)}) async-start(f32[8,4,8,128]{3,2,1,0:T(8,128)} %bitcast.15), calls=%async_computation.5 | async-start | bytes 262144 | tf_op jit(solution)/shard_map/all_to_all | solution.py:420
  129.6 0.5 pick.1.small_ref
  130.1 7.4 %all-to-all-done.5.pieces_ref = f32[8,4,8,128]{3,2,1,0:T(8,128)S(1)} async-done(((f32[8,4,8,128]{3,2,1,0:T(8,128)}), f32[8,4,8,128]{3,2,1,0:T(8,128)S(1)}, u32[]{:S(2)}, u32[]{:S(2)}) %all-to-all-start.5) | async-done | bytes 131104 | tf_op jit(solution)/shard_map/all_to_all | solution.py:420
  137.5 0.0 copy-done.1
  137.5 2.2 %lift.1 = f32[512,128]{1,0:T(8,128)} custom-call(f32[8,4,8,128]{3,2,1,0:T(8,128)S(1)} %all-to-all-done.5.pieces_ref, f32[32,128]{1,0:T(8,128)S(1)} %get-tuple-element.28.held_modes_ref, f32[4096,128]{1,0:T(8,128)S(1)} %bitcast.26, f32[8,128]{1,0:T(8,128)S(1)} %pick.1.small_ref), custom_call_target="tpu_custom_call" | custom-call | tf_op jit(solution)/shard_map/lift/pallas_call | solution.py:478
  139.7 7.9 %all-to-all-start.6 = ((f32[128,4,128]{2,1,0:T(4,128)}), f32[128,4,128]{2,1,0:T(4,128)S(1)}, u32[]{:S(2)}, u32[]{:S(2)}) async-start(f32[128,4,128]{2,1,0:T(4,128)} %bitcast.16), calls=%async_computation.6 | async-start | bytes 524288 | tf_op jit(solution)/shard_map/all_to_all | solution.py:420
  147.7 3.0 %grad.1 = f32[4096,128]{1,0:T(8,128)} custom-call(f32[8,4,8,128]{3,2,1,0:T(8,128)S(1)} %all-to-all-done.5.pieces_ref, f32[32,128]{1,0:T(8,128)S(1)} %get-tuple-element.28.held_modes_ref, f32[3,32]{1,0:T(4,128)S(1)} %bitcast.40), custom_call_target="tpu_custom_call" | custom-call | tf_op jit(solution)/shard_map/grad/pallas_call | solution.py:479
  150.7 9.8 %all-to-all-done.6 = f32[128,4,128]{2,1,0:T(4,128)S(1)} async-done(((f32[128,4,128]{2,1,0:T(4,128)}), f32[128,4,128]{2,1,0:T(4,128)S(1)}, u32[]{:S(2)}, u32[]{:S(2)}) %all-to-all-start.6) | async-done | bytes 262176 | tf_op jit(solution)/shard_map/all_to_all | solution.py:420
  160.5 0.1 reduce_sum.9.sum_ref
  160.6 0.8 last.1
Async XLA Ops:
  0.6 0.9 copy-start.2
  1.6 0.7 copy-start.9
  34.2 1.6 copy-start
  35.8 0.7 copy-start.6
  36.5 21.8 %copy-start.5 = (f32[32,32]{1,0:T(8,128)S(1)}, f32[32,32]{1,0:T(8,128)}, u32[]{:S(2)}) copy-start(f32[32,32]{1,0:T(8,128)} %mix_ref.3) | copy-start | bytes 12292
  36.5 21.8 %copy-start.7 = (f32[32,3]{0,1:T(4,128)S(1)}, f32[32,3]{0,1:T(4,128)}, u32[]{:S(2)}) copy-start(f32[32,3]{0,1:T(4,128)} %param.12) | copy-start | bytes 1156
  36.5 21.8 %copy-start.8 = (s32[8,16]{1,0:T(8,128)S(1)}, s32[8,16]{1,0:T(8,128)}, u32[]{:S(2)}) copy-start(s32[8,16]{1,0:T(8,128)} %mask_ref.1) | copy-start | bytes 1540
  36.5 21.8 %copy-start.10 = (f32[3,32]{1,0:T(4,128)S(1)}, f32[3,32]{1,0:T(4,128)}, u32[]{:S(2)}) copy-start(f32[3,32]{1,0:T(4,128)} %proj_ref.1) | copy-start | bytes 1156
  36.5 47.3 %copy-start.3 = (f32[1,3,8,16,128]{4,3,2,1,0:T(8,128)S(1)}, f32[1,3,8,16,128]{4,3,2,1,0:T(8,128)}, u32[]{:S(2)}) copy-start(f32[1,3,8,16,128]{4,3,2,1,0:T(8,128)} %param.8) | copy-start | bytes 589828
  36.5 47.3 %copy-start.4 = (f32[1,3,8,16,128]{4,3,2,1,0:T(8,128)S(1)}, f32[1,3,8,16,128]{4,3,2,1,0:T(8,128)}, u32[]{:S(2)}) copy-start(f32[1,3,8,16,128]{4,3,2,1,0:T(8,128)} %param.9) | copy-start | bytes 589828
  51.1 32.8 %all-to-all-start.3 = ((f32[128,16,128]{2,1,0:T(8,128)}), f32[128,16,128]{2,1,0:T(8,128)S(1)}, u32[]{:S(2)}, u32[]{:S(2)}) async-start(f32[128,16,128]{2,1,0:T(8,128)} %bitcast.10), calls=%async_computation.3 | async-start | bytes 2097152 | tf_op jit(solution)/shard_map/all_to_all | solution.py:420
  90.7 46.8 %copy-start.1 = (f32[2,4,32,2,1024]{4,3,2,1,0:T(2,128)S(1)}, f32[2,4,32,2,1024]{4,3,2,1,0:T(2,128)}, u32[]{:S(2)}) copy-start(f32[2,4,32,2,1024]{4,3,2,1,0:T(2,128)} %param.14) | copy-start | bytes 6291460
  124.9 12.6 %all-to-all-start.5 = ((f32[8,4,8,128]{3,2,1,0:T(8,128)}), f32[8,4,8,128]{3,2,1,0:T(8,128)S(1)}, u32[]{:S(2)}, u32[]{:S(2)}) async-start(f32[8,4,8,128]{3,2,1,0:T(8,128)} %bitcast.15), calls=%async_computation.5 | async-start | bytes 262144 | tf_op jit(solution)/shard_map/all_to_all | solution.py:420
  139.7 20.7 %all-to-all-start.6 = ((f32[128,4,128]{2,1,0:T(4,128)}), f32[128,4,128]{2,1,0:T(4,128)S(1)}, u32[]{:S(2)}, u32[]{:S(2)}) async-start(f32[128,4,128]{2,1,0:T(4,128)} %bitcast.16), calls=%async_computation.6 | async-start | bytes 524288 | tf_op jit(solution)/shard_map/all_to_all | solution.py:420

commit v5 on v4

--- a/solution.py
+++ b/solution.py
@@ -201,7 +201,10 @@
             regroup([held_ref[pl.ds(256 * part + o, 32, stride=8), :] for o in range(8)])
         )
     lane = iota((256, 128), 1)
-    table = split(wave(rows_waves(freq_ref[0:1, :], lambda part: 32 * (lane // 32 - part)))[:, :64])
+    table = wave(rows_waves(freq_ref[0:1, :], lambda part: 32 * (lane // 32 % 2 - part)))
+    high = table.astype(BF16)
+    both = jnp.where(lane < 64, high.astype(F32), table - high.astype(F32)).astype(BF16)
+    high = high[:, :64]
     copies = []
     for pair in range(4):
         wide = jnp.concatenate(
@@ -211,7 +214,10 @@
             ],
             axis=1,
         )
-        result = dot3(table, wide)
+        wide_high, wide_low = split(wide)
+        result = mul(high, wide_low, NN) + mul(
+            both, jnp.concatenate([wide_high, wide_high], axis=0), NN
+        )
         for k in range(2):
             start = 256 * (2 * pair + k)
             out_ref[start : start + 256, :] = result[:, 128 * k : 128 * k + 128]
@@ -291,7 +297,7 @@
     lax.fori_loop(0, 8, plane, 0, unroll=8)
 
 
-def pick_kernel(point_grad, proj_grad, small_ref):
+def pick_small(point_grad, proj_grad):
     same = iota((64, 512), 0) % 16 == iota((64, 512), 1) % 16
     pick = jnp.where(iota((8, 64), 0) == iota((8, 64), 1) // 16, 1.0, 0.0)
     total = jnp.zeros((8, 128), F32)
@@ -299,7 +305,7 @@
         kept = dot3(pick, jnp.where(same, ref[...], 0.0))
         place = jnp.where(iota((512, 128), 0) // 16 + offset == iota((512, 128), 1), 1.0, 0.0)
         total = total + dot3(kept, place)
-    small_ref[...] = total
+    return total
 
 
 def reduce_kernel(freq_ref, pieces_ref, out_ref, held_ref):
@@ -324,7 +330,7 @@
     return mul(jnp.concatenate(split(grads.T), axis=1), tile, NN)
 
 
-def lift_kernel(pieces_ref, held_modes_ref, weight_ref, small_ref, sum_ref):
+def lift_kernel(pieces_ref, held_modes_ref, weight_ref, point_grad, proj_grad, sum_ref):
     tile = jnp.where(iota((32, 128), 0) == iota((32, 128), 1) % 32, SCALE, 0.0).astype(BF16)
     tile = jnp.concatenate([tile, tile], axis=0)
     even = iota((8, 128), 0) % 2 == 0
@@ -361,7 +367,7 @@
                 keepdims=True,
             )
         )
-    total = small_ref[...] + jnp.concatenate(lines + [jnp.zeros((5, 128), F32)], axis=0)
+    total = pick_small(point_grad, proj_grad) + jnp.concatenate(lines + [jnp.zeros((5, 128), F32)], axis=0)
     total = jnp.where(iota((8, 128), 0) < 4, total, pltpu.roll(total, 4, 0))
     for target in range(64):
         sum_ref[8 * target : 8 * target + 8, :] = total
@@ -469,13 +475,14 @@
     pieces, point_grad, proj_grad = call(
         grid_kernel, (array(2048, 128), array(64, 512), array(64, 512)), name="grid"
     )(freq, pieces, field, target, mask, point, proj)
-    small = call(pick_kernel, array(8, 128), name="pick")(point_grad, proj_grad)
     pieces = exchange(pieces.reshape(128, 16, 128), ("py", "px")).reshape(2048, 128)
     pieces = call(reduce_kernel, array(256, 128), [pltpu.VMEM((512, 128), F32)], name="reduce")(
         freq, pieces
     )
     pieces = exchange(pieces.reshape(8, 4, 8, 128), "py")
-    sums = call(lift_kernel, array(512, 128), name="lift")(pieces, held_modes, weight, small)
+    sums = call(lift_kernel, array(512, 128), name="lift")(
+        pieces, held_modes, weight, point_grad, proj_grad
+    )
     grad = call(grad_kernel, array(4096, 128), name="grad")(pieces, held_modes, lift_rows)
     sums = exchange(sums.reshape(128, 4, 128), ("px", "py"))
     sums = jnp.sum(sums, axis=0)

time: 162 us -> 161 us (level)
  blocking collectives: 73.5 us -> 85.9 us
  waiting for transfers between devices: 42.4 us -> 35 us
  starting transfers between devices: 19.8 us -> 14.4 us
    all_to_all x4 -> x5, blocking collectives: 73.5 us -> 85.9 us  [exchange(): return lax.all_to_all(value, axes, split_axis=0, concat_axis=0, tiled=True)]
    all_to_all x3 -> x2, waiting for transfers between devices: 42.4 us -> 35 us  [exchange(): return lax.all_to_all(value, axes, split_axis=0, concat_axis=0, tiled=True)]
    all_to_all x3 -> x2, starting transfers between devices: 19.8 us -> 14.4 us  [exchange(): return lax.all_to_all(value, axes, split_axis=0, concat_axis=0, tiled=True)]
  transfers between devices with their start and end apart: 3 -> 2, of which waited for: 3 -> 2; matrix products, arithmetic and copies ran while one was open for 0% -> 0% of each run, Pallas kernels for 2% -> 2%
where the time goes in v5:
time: 161 us; the launch traced here: 160 us
  blocking collectives  85.9 us (53%)
  waiting for transfers between devices  35 us (22%)
  Pallas kernels  20.1 us (12%)
  starting transfers between devices  14.4 us (9%)
  local copies, waits for them, and re-layouts  3.91 us (2%)
    all_to_all x5, blocking collectives, exchange(): return lax.all_to_all(value, axes, split_axis=0, concat_axis=0, tiled=True)  85.9 us
    all_to_all x2, waiting for transfers between devices, exchange(): return lax.all_to_all(value, axes, split_axis=0, concat_axis=0, tiled=True)  35 us
    all_to_all x2, starting transfers between devices, exchange(): return lax.all_to_all(value, axes, split_axis=0, concat_axis=0, tiled=True)  14.4 us
    pallas_call x1, Pallas kernels, body(): call(grid_kernel, (array(2048, 128), array(64, 512), array(64, 512)), nam...  6.9 us
    unnamed x22, local copies, waits for them, and re-layouts  3.91 us
  transfers between devices with their start and end apart: 2, of which 2 were waited for; matrix products, arithmetic and copies ran while one was open for 0% of the time, Pallas kernels for 2%

profile of v5, /device:TPU:8, one launch (start us, length us, event | category | flops | bytes accessed | tf_op | source)
XLA Modules:
  0.0 160.1 jit_solution(11982809015255728513)
XLA Ops:
  0.6 0.0 copy-start.2
  0.6 0.9 copy-done.2
  1.6 0.0 copy-start.9
  1.6 0.7 copy-done.9
  2.2 0.8 input_depth.1
  3.0 17.3 %all_to_all.35 = f32[16,16,128]{2,1,0:T(8,128)S(1)} all-to-all(f32[16,16,128]{2,1,0:T(8,128)S(1)} %bitcast.37), channel_id=1, replica_groups=mesh['seed'=2,'px'=16,'py'=8] {'px'}, dimensions={0} | all-to-all | bytes 262144 | tf_op jit(solution)/shard_map/all_to_all | solution.py:426
  20.3 0.3 input_rows.1
  20.7 13.5 %all_to_all.36 = f32[8,8,128]{2,1,0:T(8,128)S(1)} all-to-all(f32[8,8,128]{2,1,0:T(8,128)S(1)} %bitcast.38), channel_id=1, replica_groups=mesh['seed'=2,'px'=16,'py'=8] {'py'}, dimensions={0} | all-to-all | bytes 65536 | tf_op jit(solution)/shard_map/all_to_all | solution.py:426
  34.2 0.0 copy-start
  34.2 1.6 copy-done
  35.8 0.0 copy-start.6
  35.8 0.7 copy-done.6
  36.5 0.0 copy-start.5
  36.5 0.0 copy-start.7
  36.5 0.0 copy-start.8
  36.5 0.0 copy-start.10
  36.5 0.0 copy-start.3
  36.5 0.0 copy-start.4
  36.5 2.1 %mix.1 = (f32[32,128]{1,0:T(8,128)S(1)}, f32[8,4,8,128]{3,2,1,0:T(8,128)S(1)}) custom-call(s32[8,128]{1,0:T(8,128)S(1)} %get-tuple-element.19.freq_ref, f32[64,128]{1,0:T(8,128)S(1)} %bitcast.36, f32[3,32]{1,0:T(4,128)S(1)} %bitcast.39, f32[4096,128]{1,0:T(8,128)S(1)} %bitcast.25), custom_call_target="tpu_custom_call" | custom-call | tf_op jit(solution)/shard_map/mix/pallas_call | solution.py:453
  38.6 10.3 %all_to_all.37 = f32[8,4,8,128]{3,2,1,0:T(8,128)S(1)} all-to-all(f32[8,4,8,128]{3,2,1,0:T(8,128)S(1)} %get-tuple-element.21), channel_id=1, replica_groups=mesh['seed'=2,'px'=16,'py'=8] {'py'}, dimensions={0} | all-to-all | bytes 262144 | tf_op jit(solution)/shard_map/all_to_all | solution.py:426
  48.9 2.1 %expand.1 = (f32[2048,128]{1,0:T(8,128)}, f32[8,128]{1,0:T(8,128)S(1)}) custom-call(s32[8,128]{1,0:T(8,128)S(1)} %get-tuple-element.19.freq_ref, f32[256,128]{1,0:T(8,128)S(1)} %bitcast.33), custom_call_target="tpu_custom_call" | custom-call | tf_op jit(solution)/shard_map/expand/pallas_call | solution.py:460
  51.0 7.2 %all-to-all-start.3 = ((f32[128,16,128]{2,1,0:T(8,128)}), f32[128,16,128]{2,1,0:T(8,128)S(1)}, u32[]{:S(2)}, u32[]{:S(2)}) async-start(f32[128,16,128]{2,1,0:T(8,128)} %bitcast.10), calls=%async_computation.3 | async-start | bytes 2097152 | tf_op jit(solution)/shard_map/all_to_all | solution.py:426
  58.2 0.0 copy-done.5
  58.2 0.0 copy-done.7
  58.2 0.0 copy-done.8
  58.2 0.0 copy-done.10
  58.2 0.3 tables.1
  58.5 25.2 %all-to-all-done.3 = f32[128,16,128]{2,1,0:T(8,128)S(1)} async-done(((f32[128,16,128]{2,1,0:T(8,128)}), f32[128,16,128]{2,1,0:T(8,128)S(1)}, u32[]{:S(2)}, u32[]{:S(2)}) %all-to-all-start.3) | async-done | bytes 1048608 | tf_op jit(solution)/shard_map/all_to_all | solution.py:426
  83.7 0.0 copy-done.3
  83.7 0.0 copy-done.4
  83.7 6.9 %grid.1 = (f32[2048,128]{1,0:T(8,128)S(1)}, f32[64,512]{1,0:T(8,128)S(1)}, f32[64,512]{1,0:T(8,128)S(1)}) custom-call(s32[8,128]{1,0:T(8,128)S(1)} %get-tuple-element.19.freq_ref, f32[2048,128]{1,0:T(8,128)S(1)} %bitcast.27, f32[3,8,16,128]{3,2,1,0:T(8,128)S(1)} %bitcast.31, f32[3,8,16,128]{3,2,1,0:T(8,128)S(1)} %bitcast.35, ...), custom_call_target="tpu_custom_call" | custom-call | tf_op jit(solution)/shard_map/grid/pallas_call | solution.py:475
  90.6 0.0 copy-start.1
  90.7 32.4 %all_to_all.38 = f32[128,16,128]{2,1,0:T(8,128)S(1)} all-to-all(f32[128,16,128]{2,1,0:T(8,128)S(1)} %bitcast.29), channel_id=1, replica_groups=mesh['seed'=2,'px'=16,'py'=8] {'py','px'}, dimensions={0} | all-to-all | bytes 2097152 | tf_op jit(solution)/shard_map/all_to_all | solution.py:426
  123.0 1.2 reduce.1
  124.2 12.4 %all_to_all.39.pieces_ref = f32[8,4,8,128]{3,2,1,0:T(8,128)S(1)} all-to-all(f32[8,4,8,128]{3,2,1,0:T(8,128)S(1)} %bitcast.32), channel_id=1, replica_groups=mesh['seed'=2,'px'=16,'py'=8] {'py'}, dimensions={0} | all-to-all | bytes 262144 | tf_op jit(solution)/shard_map/all_to_all | solution.py:426
  136.5 0.0 copy-done.1
  136.5 2.6 %lift.1 = f32[512,128]{1,0:T(8,128)} custom-call(f32[8,4,8,128]{3,2,1,0:T(8,128)S(1)} %all_to_all.39.pieces_ref, f32[32,128]{1,0:T(8,128)S(1)} %get-tuple-element.28.held_modes_ref, f32[4096,128]{1,0:T(8,128)S(1)} %bitcast.26, f32[64,512]{1,0:T(8,128)S(1)} %get-tuple-element.29.point_grad, f32[64,512]{1,0:T(8,128)S(1)} %get-tuple-element.30.proj_grad), custom_call_target="tpu_custom_call" | custom-call | tf_op jit(solution)/shard_map/lift/pallas_call | solution.py:483
  139.2 7.2 %all-to-all-start.6 = ((f32[128,4,128]{2,1,0:T(4,128)}), f32[128,4,128]{2,1,0:T(4,128)S(1)}, u32[]{:S(2)}, u32[]{:S(2)}) async-start(f32[128,4,128]{2,1,0:T(4,128)} %bitcast.16), calls=%async_computation.6 | async-start | bytes 524288 | tf_op jit(solution)/shard_map/all_to_all | solution.py:426
  146.4 3.0 %grad.1 = f32[4096,128]{1,0:T(8,128)} custom-call(f32[8,4,8,128]{3,2,1,0:T(8,128)S(1)} %all_to_all.39.pieces_ref, f32[32,128]{1,0:T(8,128)S(1)} %get-tuple-element.28.held_modes_ref, f32[3,32]{1,0:T(4,128)S(1)} %bitcast.41), custom_call_target="tpu_custom_call" | custom-call | tf_op jit(solution)/shard_map/grad/pallas_call | solution.py:486
  149.4 9.8 %all-to-all-done.6 = f32[128,4,128]{2,1,0:T(4,128)S(1)} async-done(((f32[128,4,128]{2,1,0:T(4,128)}), f32[128,4,128]{2,1,0:T(4,128)S(1)}, u32[]{:S(2)}, u32[]{:S(2)}) %all-to-all-start.6) | async-done | bytes 262176 | tf_op jit(solution)/shard_map/all_to_all | solution.py:426
  159.2 0.1 reduce_sum.9.sum_ref
  159.4 0.8 last.1
Async XLA Ops:
  0.6 0.9 copy-start.2
  1.6 0.7 copy-start.9
  34.2 1.6 copy-start
  35.8 0.7 copy-start.6
  36.5 21.7 %copy-start.5 = (f32[32,32]{1,0:T(8,128)S(1)}, f32[32,32]{1,0:T(8,128)}, u32[]{:S(2)}) copy-start(f32[32,32]{1,0:T(8,128)} %mix_ref.3) | copy-start | bytes 12292
  36.5 21.7 %copy-start.7 = (f32[32,3]{0,1:T(4,128)S(1)}, f32[32,3]{0,1:T(4,128)}, u32[]{:S(2)}) copy-start(f32[32,3]{0,1:T(4,128)} %param.12) | copy-start | bytes 1156
  36.5 21.7 %copy-start.8 = (s32[8,16]{1,0:T(8,128)S(1)}, s32[8,16]{1,0:T(8,128)}, u32[]{:S(2)}) copy-start(s32[8,16]{1,0:T(8,128)} %mask_ref.1) | copy-start | bytes 1540
  36.5 21.7 %copy-start.10 = (f32[3,32]{1,0:T(4,128)S(1)}, f32[3,32]{1,0:T(4,128)}, u32[]{:S(2)}) copy-start(f32[3,32]{1,0:T(4,128)} %proj_ref.1) | copy-start | bytes 1156
  36.5 47.3 %copy-start.3 = (f32[1,3,8,16,128]{4,3,2,1,0:T(8,128)S(1)}, f32[1,3,8,16,128]{4,3,2,1,0:T(8,128)}, u32[]{:S(2)}) copy-start(f32[1,3,8,16,128]{4,3,2,1,0:T(8,128)} %param.8) | copy-start | bytes 589828
  36.5 47.2 %copy-start.4 = (f32[1,3,8,16,128]{4,3,2,1,0:T(8,128)S(1)}, f32[1,3,8,16,128]{4,3,2,1,0:T(8,128)}, u32[]{:S(2)}) copy-start(f32[1,3,8,16,128]{4,3,2,1,0:T(8,128)} %param.9) | copy-start | bytes 589828
  51.0 32.8 %all-to-all-start.3 = ((f32[128,16,128]{2,1,0:T(8,128)}), f32[128,16,128]{2,1,0:T(8,128)S(1)}, u32[]{:S(2)}, u32[]{:S(2)}) async-start(f32[128,16,128]{2,1,0:T(8,128)} %bitcast.10), calls=%async_computation.3 | async-start | bytes 2097152 | tf_op jit(solution)/shard_map/all_to_all | solution.py:426
  90.6 45.9 %copy-start.1 = (f32[2,4,32,2,1024]{4,3,2,1,0:T(2,128)S(1)}, f32[2,4,32,2,1024]{4,3,2,1,0:T(2,128)}, u32[]{:S(2)}) copy-start(f32[2,4,32,2,1024]{4,3,2,1,0:T(2,128)} %param.14) | copy-start | bytes 6291460
  139.2 20.0 %all-to-all-start.6 = ((f32[128,4,128]{2,1,0:T(4,128)}), f32[128,4,128]{2,1,0:T(4,128)S(1)}, u32[]{:S(2)}, u32[]{:S(2)}) async-start(f32[128,4,128]{2,1,0:T(4,128)} %bitcast.16), calls=%async_computation.6 | async-start | bytes 524288 | tf_op jit(solution)/shard_map/all_to_all | solution.py:426

commit v6 on v5

--- a/solution.py
+++ b/solution.py
@@ -54,7 +54,7 @@
 
 
 def dot2k(left, right):
-    left_high, left_low = split(left)
+    left_high, left_low = left if isinstance(left, tuple) else split(left)
     right_high, right_low = right if isinstance(right, tuple) else split(right)
     wide = jnp.concatenate([left_high, left_low], axis=1)
     tall = jnp.concatenate([right_high, right_high], axis=0)
@@ -159,8 +159,8 @@
     shape = (N, 128)
     lane = iota(shape, 1)
     turns = iota(shape, 0) * freq_ref[1:2, :]
-    held_ref[:, :128] = dot3(rows, wave(turns + 32 * (lane // 64)))
-    held_ref[:, 128:] = dot3(rows, wave(turns + 32 * (lane // 64) - 32))
+    held_ref[:, :128] = dot2k(rows, wave(turns + 32 * (lane // 64)))
+    held_ref[:, 128:] = dot2k(rows, wave(turns + 32 * (lane // 64) - 32))
     first_slot = iota((4, 128), 1) // 32 % 2 == 0
     held_modes_ref[...] = jnp.zeros((32, 128), F32)
     for channel in range(3):
@@ -192,7 +192,13 @@
 
 
 def expand(freq_ref, pieces_ref, out_hbm, mark_ref, held_ref, out_ref, sems):
-    result = dot3(pieces_ref[...], plane_waves(freq_ref), NT)
+    high, low = split(pieces_ref[...])
+    table_high, table_low = plane_waves(freq_ref)
+    result = mul(high, table_low, NT) + mul(
+        jnp.concatenate([high, low], axis=1),
+        jnp.concatenate([table_high, table_high], axis=1),
+        NT,
+    )
     held_ref[:256, :] = result[:, :128]
     held_ref[256:, :] = result[:, 128:]
     parts = []

time: 161 us -> 161 us (level)
  no operation moved by 1% of the time
where the time goes in v6:
time: 161 us; the launch traced here: 160 us
  blocking collectives  85.9 us (53%)
  waiting for transfers between devices  35 us (22%)
  Pallas kernels  20 us (12%)
  starting transfers between devices  14.4 us (9%)
  local copies, waits for them, and re-layouts  3.91 us (2%)
    all_to_all x5, blocking collectives, exchange(): return lax.all_to_all(value, axes, split_axis=0, concat_axis=0, tiled=True)  85.9 us
    all_to_all x2, waiting for transfers between devices, exchange(): return lax.all_to_all(value, axes, split_axis=0, concat_axis=0, tiled=True)  35 us
    all_to_all x2, starting transfers between devices, exchange(): return lax.all_to_all(value, axes, split_axis=0, concat_axis=0, tiled=True)  14.4 us
    pallas_call x1, Pallas kernels, body(): call(grid_kernel, (array(2048, 128), array(64, 512), array(64, 512)), nam...  6.9 us
    unnamed x22, local copies, waits for them, and re-layouts  3.91 us
  transfers between devices with their start and end apart: 2, of which 2 were waited for; matrix products, arithmetic and copies ran while one was open for 0% of the time, Pallas kernels for 2%

profile of v6, /device:TPU:8, one launch (start us, length us, event | category | flops | bytes accessed | tf_op | source)
XLA Modules:
  0.0 160.0 jit_solution(3188232779840044984)
XLA Ops:
  0.6 0.0 copy-start.2
  0.6 0.9 copy-done.2
  1.6 0.0 copy-start.9
  1.6 0.7 copy-done.9
  2.2 0.8 input_depth.1
  3.0 17.3 %all_to_all.35 = f32[16,16,128]{2,1,0:T(8,128)S(1)} all-to-all(f32[16,16,128]{2,1,0:T(8,128)S(1)} %bitcast.37), channel_id=1, replica_groups=mesh['seed'=2,'px'=16,'py'=8] {'px'}, dimensions={0} | all-to-all | bytes 262144 | tf_op jit(solution)/shard_map/all_to_all | solution.py:432
  20.3 0.3 input_rows.1
  20.7 13.5 %all_to_all.36 = f32[8,8,128]{2,1,0:T(8,128)S(1)} all-to-all(f32[8,8,128]{2,1,0:T(8,128)S(1)} %bitcast.38), channel_id=1, replica_groups=mesh['seed'=2,'px'=16,'py'=8] {'py'}, dimensions={0} | all-to-all | bytes 65536 | tf_op jit(solution)/shard_map/all_to_all | solution.py:432
  34.2 0.0 copy-start
  34.2 1.6 copy-done
  35.8 0.0 copy-start.6
  35.8 0.7 copy-done.6
  36.5 0.0 copy-start.5
  36.5 0.0 copy-start.7
  36.5 0.0 copy-start.8
  36.5 0.0 copy-start.10
  36.5 0.0 copy-start.3
  36.5 0.0 copy-start.4
  36.5 2.1 %mix.1 = (f32[32,128]{1,0:T(8,128)S(1)}, f32[8,4,8,128]{3,2,1,0:T(8,128)S(1)}) custom-call(s32[8,128]{1,0:T(8,128)S(1)} %get-tuple-element.19.freq_ref, f32[64,128]{1,0:T(8,128)S(1)} %bitcast.36, f32[3,32]{1,0:T(4,128)S(1)} %bitcast.39, f32[4096,128]{1,0:T(8,128)S(1)} %bitcast.25), custom_call_target="tpu_custom_call" | custom-call | tf_op jit(solution)/shard_map/mix/pallas_call | solution.py:459
  38.6 10.3 %all_to_all.37 = f32[8,4,8,128]{3,2,1,0:T(8,128)S(1)} all-to-all(f32[8,4,8,128]{3,2,1,0:T(8,128)S(1)} %get-tuple-element.21), channel_id=1, replica_groups=mesh['seed'=2,'px'=16,'py'=8] {'py'}, dimensions={0} | all-to-all | bytes 262144 | tf_op jit(solution)/shard_map/all_to_all | solution.py:432
  48.9 2.0 %expand.1 = (f32[2048,128]{1,0:T(8,128)}, f32[8,128]{1,0:T(8,128)S(1)}) custom-call(s32[8,128]{1,0:T(8,128)S(1)} %get-tuple-element.19.freq_ref, f32[256,128]{1,0:T(8,128)S(1)} %bitcast.33), custom_call_target="tpu_custom_call" | custom-call | tf_op jit(solution)/shard_map/expand/pallas_call | solution.py:466
  50.9 7.2 %all-to-all-start.3 = ((f32[128,16,128]{2,1,0:T(8,128)}), f32[128,16,128]{2,1,0:T(8,128)S(1)}, u32[]{:S(2)}, u32[]{:S(2)}) async-start(f32[128,16,128]{2,1,0:T(8,128)} %bitcast.10), calls=%async_computation.3 | async-start | bytes 2097152 | tf_op jit(solution)/shard_map/all_to_all | solution.py:432
  58.1 0.0 copy-done.5
  58.1 0.0 copy-done.7
  58.1 0.0 copy-done.8
  58.1 0.0 copy-done.10
  58.1 0.3 tables.1
  58.4 25.2 %all-to-all-done.3 = f32[128,16,128]{2,1,0:T(8,128)S(1)} async-done(((f32[128,16,128]{2,1,0:T(8,128)}), f32[128,16,128]{2,1,0:T(8,128)S(1)}, u32[]{:S(2)}, u32[]{:S(2)}) %all-to-all-start.3) | async-done | bytes 1048608 | tf_op jit(solution)/shard_map/all_to_all | solution.py:432
  83.7 0.0 copy-done.3
  83.7 0.0 copy-done.4
  83.7 6.9 %grid.1 = (f32[2048,128]{1,0:T(8,128)S(1)}, f32[64,512]{1,0:T(8,128)S(1)}, f32[64,512]{1,0:T(8,128)S(1)}) custom-call(s32[8,128]{1,0:T(8,128)S(1)} %get-tuple-element.19.freq_ref, f32[2048,128]{1,0:T(8,128)S(1)} %bitcast.27, f32[3,8,16,128]{3,2,1,0:T(8,128)S(1)} %bitcast.31, f32[3,8,16,128]{3,2,1,0:T(8,128)S(1)} %bitcast.35, ...), custom_call_target="tpu_custom_call" | custom-call | tf_op jit(solution)/shard_map/grid/pallas_call | solution.py:481
  90.6 0.0 copy-start.1
  90.6 32.4 %all_to_all.38 = f32[128,16,128]{2,1,0:T(8,128)S(1)} all-to-all(f32[128,16,128]{2,1,0:T(8,128)S(1)} %bitcast.29), channel_id=1, replica_groups=mesh['seed'=2,'px'=16,'py'=8] {'py','px'}, dimensions={0} | all-to-all | bytes 2097152 | tf_op jit(solution)/shard_map/all_to_all | solution.py:432
  122.9 1.2 reduce.1
  124.1 12.4 %all_to_all.39.pieces_ref = f32[8,4,8,128]{3,2,1,0:T(8,128)S(1)} all-to-all(f32[8,4,8,128]{3,2,1,0:T(8,128)S(1)} %bitcast.32), channel_id=1, replica_groups=mesh['seed'=2,'px'=16,'py'=8] {'py'}, dimensions={0} | all-to-all | bytes 262144 | tf_op jit(solution)/shard_map/all_to_all | solution.py:432
  136.5 0.0 copy-done.1
  136.5 2.6 %lift.1 = f32[512,128]{1,0:T(8,128)} custom-call(f32[8,4,8,128]{3,2,1,0:T(8,128)S(1)} %all_to_all.39.pieces_ref, f32[32,128]{1,0:T(8,128)S(1)} %get-tuple-element.28.held_modes_ref, f32[4096,128]{1,0:T(8,128)S(1)} %bitcast.26, f32[64,512]{1,0:T(8,128)S(1)} %get-tuple-element.29.point_grad, f32[64,512]{1,0:T(8,128)S(1)} %get-tuple-element.30.proj_grad), custom_call_target="tpu_custom_call" | custom-call | tf_op jit(solution)/shard_map/lift/pallas_call | solution.py:489
  139.1 7.2 %all-to-all-start.6 = ((f32[128,4,128]{2,1,0:T(4,128)}), f32[128,4,128]{2,1,0:T(4,128)S(1)}, u32[]{:S(2)}, u32[]{:S(2)}) async-start(f32[128,4,128]{2,1,0:T(4,128)} %bitcast.16), calls=%async_computation.6 | async-start | bytes 524288 | tf_op jit(solution)/shard_map/all_to_all | solution.py:432
  146.3 3.0 %grad.1 = f32[4096,128]{1,0:T(8,128)} custom-call(f32[8,4,8,128]{3,2,1,0:T(8,128)S(1)} %all_to_all.39.pieces_ref, f32[32,128]{1,0:T(8,128)S(1)} %get-tuple-element.28.held_modes_ref, f32[3,32]{1,0:T(4,128)S(1)} %bitcast.41), custom_call_target="tpu_custom_call" | custom-call | tf_op jit(solution)/shard_map/grad/pallas_call | solution.py:492
  149.4 9.8 %all-to-all-done.6 = f32[128,4,128]{2,1,0:T(4,128)S(1)} async-done(((f32[128,4,128]{2,1,0:T(4,128)}), f32[128,4,128]{2,1,0:T(4,128)S(1)}, u32[]{:S(2)}, u32[]{:S(2)}) %all-to-all-start.6) | async-done | bytes 262176 | tf_op jit(solution)/shard_map/all_to_all | solution.py:432
  159.1 0.1 reduce_sum.9.sum_ref
  159.3 0.8 last.1
Async XLA Ops:
  0.6 0.9 copy-start.2
  1.6 0.7 copy-start.9
  34.2 1.6 copy-start
  35.8 0.7 copy-start.6
  36.5 21.6 %copy-start.5 = (f32[32,32]{1,0:T(8,128)S(1)}, f32[32,32]{1,0:T(8,128)}, u32[]{:S(2)}) copy-start(f32[32,32]{1,0:T(8,128)} %mix_ref.3) | copy-start | bytes 12292
  36.5 21.6 %copy-start.7 = (f32[32,3]{0,1:T(4,128)S(1)}, f32[32,3]{0,1:T(4,128)}, u32[]{:S(2)}) copy-start(f32[32,3]{0,1:T(4,128)} %param.12) | copy-start | bytes 1156
  36.5 21.6 %copy-start.8 = (s32[8,16]{1,0:T(8,128)S(1)}, s32[8,16]{1,0:T(8,128)}, u32[]{:S(2)}) copy-start(s32[8,16]{1,0:T(8,128)} %mask_ref.1) | copy-start | bytes 1540
  36.5 21.6 %copy-start.10 = (f32[3,32]{1,0:T(4,128)S(1)}, f32[3,32]{1,0:T(4,128)}, u32[]{:S(2)}) copy-start(f32[3,32]{1,0:T(4,128)} %proj_ref.1) | copy-start | bytes 1156
  36.5 47.2 %copy-start.3 = (f32[1,3,8,16,128]{4,3,2,1,0:T(8,128)S(1)}, f32[1,3,8,16,128]{4,3,2,1,0:T(8,128)}, u32[]{:S(2)}) copy-start(f32[1,3,8,16,128]{4,3,2,1,0:T(8,128)} %param.8) | copy-start | bytes 589828
  36.5 47.2 %copy-start.4 = (f32[1,3,8,16,128]{4,3,2,1,0:T(8,128)S(1)}, f32[1,3,8,16,128]{4,3,2,1,0:T(8,128)}, u32[]{:S(2)}) copy-start(f32[1,3,8,16,128]{4,3,2,1,0:T(8,128)} %param.9) | copy-start | bytes 589828
  50.9 32.8 %all-to-all-start.3 = ((f32[128,16,128]{2,1,0:T(8,128)}), f32[128,16,128]{2,1,0:T(8,128)S(1)}, u32[]{:S(2)}, u32[]{:S(2)}) async-start(f32[128,16,128]{2,1,0:T(8,128)} %bitcast.10), calls=%async_computation.3 | async-start | bytes 2097152 | tf_op jit(solution)/shard_map/all_to_all | solution.py:432
  90.6 45.9 %copy-start.1 = (f32[2,4,32,2,1024]{4,3,2,1,0:T(2,128)S(1)}, f32[2,4,32,2,1024]{4,3,2,1,0:T(2,128)}, u32[]{:S(2)}) copy-start(f32[2,4,32,2,1024]{4,3,2,1,0:T(2,128)} %param.14) | copy-start | bytes 6291460
  139.1 20.0 %all-to-all-start.6 = ((f32[128,4,128]{2,1,0:T(4,128)}), f32[128,4,128]{2,1,0:T(4,128)S(1)}, u32[]{:S(2)}, u32[]{:S(2)}) async-start(f32[128,4,128]{2,1,0:T(4,128)} %bitcast.16), calls=%async_computation.6 | async-start | bytes 524288 | tf_op jit(solution)/shard_map/all_to_all | solution.py:432
